TPU v7x, 512 devices: a whole 4x4x16 slice. The times are simulated.
512 devices in a mesh: group: 128 (over y_hi, z, x), tensor: 4 (over y_lo, core).
Axes of the slice: x: 4, y: 4 (y_hi: 2, y_lo: 2; y = y_hi * 2 + y_lo), z: 16, core: 2. Of those that a mesh axis runs over, the one named last changes fastest.
Arguments:
- block: bfloat16 [128, 128, 1024], P('group'), may hold values from -6 to 6
- mask: int32 [128, 128], P('group'), may hold values 0 or 1
- cache_len: int32 [128], replicated, may hold values from 128 to 1920, as said below
- cache_k: bfloat16 [128, 1024, 1024], P('group', None, 'tensor'), may hold values from -240 to 240
- cache_v: bfloat16 [128, 1024, 1024], P('group', None, 'tensor'), may hold values from -6 to 6
- w_q: bfloat16 [1024, 1024], P(None, 'tensor'), may hold values from -0.1875 to 0.1875
- b_q: bfloat16 [1024], P('tensor'), may hold values from -3 to 3
- w_k: bfloat16 [1024, 1024], P(None, 'tensor'), may hold values from -0.1875 to 0.1875
- b_k: bfloat16 [1024], P('tensor'), may hold values from -3 to 3
- w_v: bfloat16 [1024, 1024], P(None, 'tensor'), may hold values from -0.1875 to 0.1875
- b_v: bfloat16 [1024], P('tensor'), may hold values from -3 to 3
- w_o: bfloat16 [1024, 1024], P('tensor'), may hold values from -0.1875 to 0.1875
- b_o: bfloat16 [1024], replicated, may hold values from -3 to 3
- ln_gain: bfloat16 [1024], replicated, may hold values from 0.5 to 1.5
- ln_shift: bfloat16 [1024], replicated, may hold values from -3 to 3
Outputs:
- denoised: bfloat16 [128, 128, 1024], P('group')
Inputs may be any that keep to these rules, and one draw needn't show every extreme that they name: `cache_len`: in every pair exactly one request reads past its own group's slab into the partner's; the two lengths of a pair sum to at most 2048; both ends are reached in every draw.
All inputs are finite; a program needn't handle non-finite values. No bound on the sum of `mask` on one device may be relied on, other than what follows from the above.
Results may differ from a plain program's by a relative error of at most 0.03.
Values may be sent and summed in bfloat16 or wider, within the bound.
No kernel may reach another device: no remote copies, remote signals or barrier semaphores. Data moves between devices by JAX's collectives and lax.ppermute only.
A program may use at most 64 MiB of HBM per device.

v0:
```python
import jax
import jax.numpy as jnp
from jax import lax
from jax.sharding import PartitionSpec as P

HD = 64


NEG = -1e30
EPS = 1e-05


def swapped(array, axis, apart):
    return lax.ppermute(array, axis, [(i, i ^ 1 << apart) for i in range(lax.axis_size(axis))])


def project(inputs, weight, bias):
    return (
        jnp.dot(inputs, weight, preferred_element_type=jnp.float32) + bias.astype(jnp.float32)
    ).astype(jnp.bfloat16)


def layer_norm(summed, ln_gain, ln_shift):
    centre = summed - jnp.mean(summed, -1, keepdims=True)
    spread = jnp.mean(centre * centre, -1, keepdims=True)
    return (
        centre * lax.rsqrt(spread + EPS) * ln_gain.astype(jnp.float32)
        + ln_shift.astype(jnp.float32)
    ).astype(jnp.bfloat16)


def in_cache(length, req_parity, places, slab_len):
    return jnp.where(req_parity == 0, places < length, places >= 2 * slab_len - length)


def partial_attend(queries, keys, values, usable):
    row_count = queries.shape[0]
    head_count = queries.shape[1] // HD
    q_heads = queries.reshape(row_count, head_count, HD)
    k_heads = keys.reshape(keys.shape[0], head_count, HD)
    v_heads = values.reshape(values.shape[0], head_count, HD)
    scores = jnp.einsum(
        "qhd,khd->hqk", q_heads, k_heads, preferred_element_type=jnp.float32
    ) * HD ** (-0.5)
    scores = jnp.where(usable[None, None, :], scores, NEG)
    row_max = jnp.max(scores, -1)
    expo = jnp.exp(scores - row_max[:, :, None])
    row_sum = jnp.sum(expo, -1)
    summed_out = jnp.einsum(
        "hqk,khd->qhd", expo.astype(jnp.bfloat16), v_heads, preferred_element_type=jnp.float32
    )
    return (summed_out.reshape(row_count, head_count * HD), row_max, row_sum)


def body(
    block,
    mask,
    cache_len,
    cache_k,
    cache_v,
    w_q,
    b_q,
    w_k,
    b_k,
    w_v,
    b_v,
    w_o,
    b_o,
    ln_gain,
    ln_shift,
):
    tok_rows = block[0]
    own_k = cache_k[0]
    own_v = cache_v[0]
    slab_len = own_k.shape[0]
    group_idx = lax.axis_index("group")
    parity = group_idx % 2
    own_len = cache_len[group_idx]
    peer_k, peer_v = swapped((own_k, own_v), "group", 0)
    pool_k = jnp.where(
        parity == 0, jnp.concatenate([own_k, peer_k], 0), jnp.concatenate([peer_k, own_k], 0)
    )
    pool_v = jnp.where(
        parity == 0, jnp.concatenate([own_v, peer_v], 0), jnp.concatenate([peer_v, own_v], 0)
    )
    pool_usable = in_cache(own_len, parity, jnp.arange(2 * slab_len, dtype=jnp.int32), slab_len)

    def one_pass(inputs):
        queries = project(inputs, w_q, b_q)
        new_k = project(inputs, w_k, b_k)
        new_v = project(inputs, w_v, b_v)
        fresh = jnp.ones((inputs.shape[0],), bool)
        summed_out, row_max, row_sum = partial_attend(
            queries,
            jnp.concatenate([pool_k, new_k], 0),
            jnp.concatenate([pool_v, new_v], 0),
            jnp.concatenate([pool_usable, fresh], 0),
        )
        row_count = inputs.shape[0]
        head_count = row_sum.shape[0]
        attended = (
            (summed_out.reshape(row_count, head_count, HD) / row_sum.T[:, :, None])
            .reshape(row_count, head_count * HD)
            .astype(jnp.bfloat16)
        )
        partial_value = jnp.dot(attended, w_o, preferred_element_type=jnp.float32)
        summed = lax.psum(partial_value.astype(jnp.bfloat16), "tensor").astype(jnp.float32)
        return layer_norm(
            summed + b_o.astype(jnp.float32) + inputs.astype(jnp.float32), ln_gain, ln_shift
        )

    first_out = one_pass(tok_rows)
    second = jnp.where(mask[0][:, None] == 1, first_out, tok_rows)
    return one_pass(second)[None]


def solution(mesh):
    return jax.shard_map(
        body,
        mesh=mesh,
        in_specs=(
            P("group", None, None),
            P("group", None),
            P(),
            P("group", None, "tensor"),
            P("group", None, "tensor"),
            P(None, "tensor"),
            P("tensor"),
            P(None, "tensor"),
            P("tensor"),
            P(None, "tensor"),
            P("tensor"),
            P("tensor", None),
            P(),
            P(),
            P(),
        ),
        out_specs=P("group", None, None),
        check_vma=False,
    )
```

profile of v0, /device:TPU:1, one launch (start us, length us, event | category | flops | bytes accessed | tf_op | source)
XLA Modules:
  0.0 187.3 jit_solution(17652154022433314799)
XLA Ops:
  6.5 0.0 copy-start
  6.5 0.0 copy-start.4
  6.5 0.0 all-reduce.4.cloned.1.call-start
  6.5 4.1 %collective-permute-start = (bf16[1024,256]{1,0:T(8,128)(2,1)}, bf16[1024,256]{1,0:T(8,128)(2,1)S(1)}, u32[]{:S(2)}, u32[]{:S(2)}) collective-permute-start(bf16[1024,256]{1,0:T(8,128)(2,1)} %bitcast.62), channel_id=1, source_target_pairs={{0,4},{4,0},{8,12},{12,8},{16,20},{20,16},{24,28},{28,24},{32,36},... | collective-permute-start | bytes 1572872 | tf_op jit(solution)/shard_map/ppermute | solution.py:14
  10.6 1.9 %collective-permute-start.1 = (bf16[1024,256]{1,0:T(8,128)(2,1)}, bf16[1024,256]{1,0:T(8,128)(2,1)}, u32[]{:S(2)}, u32[]{:S(2)}) collective-permute-start(bf16[1024,256]{1,0:T(8,128)(2,1)} %bitcast.64), channel_id=1, source_target_pairs={{0,4},{4,0},{8,12},{12,8},{16,20},{20,16},{24,28},{28,24},{32,36},... | collective-permute-start | bytes 1572872 | tf_op jit(solution)/shard_map/ppermute | solution.py:14
  12.6 0.7 convert_element_type.86
  13.2 1.2 dynamic_slice.3
  15.1 1.4 fusion.25
  16.5 0.7 fusion.43
  17.1 0.7 convert_element_type.88
  17.8 0.1 copy.23
  17.9 0.7 convert_element_type.84
  18.6 1.4 fusion.26
  19.9 1.4 fusion.24
  21.3 0.0 collective-permute-done
  21.3 0.0 copy-start.5
  21.3 0.8 copy-done.5
  22.1 6.7 %collective-permute-done.1 = bf16[1024,256]{1,0:T(8,128)(2,1)} collective-permute-done((bf16[1024,256]{1,0:T(8,128)(2,1)}, bf16[1024,256]{1,0:T(8,128)(2,1)}, u32[]{:S(2)}, u32[]{:S(2)}) %collective-permute-start.1) | collective-permute-done | bytes 524320 | tf_op jit(solution)/shard_map/ppermute | solution.py:14
  28.8 0.0 copy-done.4
  28.8 2.4 %maximum_select_fusion = (bf16[2048,256]{1,0:T(8,128)(2,1)S(1)}, bf16[2048,256]{1,0:T(8,128)(2,1)S(1)}) fusion(bf16[1024,256]{1,0:T(8,128)(2,1)} %copy-done.5, bf16[1024,256]{1,0:T(8,128)(2,1)S(1)} %bitcast.63, pred[]{:T(512)S(6)} %eq.21, bf16[1024,256]{1,0:T(8,128)(2,1)} %bitcast.65, bf16[1024,256]{1,0:T(8,128)(2,1)} %collective-permute-done.1), kind=kLoop, calls=%fused_computation.38 | loop fusion | flops 9437184 | bytes 4194305 | tf_op jit(solution)/shard_map/jit(_where)/select_n | solution.py:83
  31.2 1.1 pad_maximum_fusion.1
  32.3 2.3 %copy.24 = bf16[2176,256]{0,1:T(8,128)(2,1)} copy(bf16[2176,256]{1,0:T(8,128)(2,1)} %pad_maximum_fusion.1) | data formatting | bytes 2228224 | tf_op jit(solution)/shard_map/concatenate | solution.py:95
  34.6 1.1 pad_maximum_fusion
  35.7 2.3 %copy.22 = bf16[2176,256]{0,1:T(8,128)(2,1)} copy(bf16[2176,256]{1,0:T(8,128)(2,1)} %pad_maximum_fusion) | data formatting | bytes 2228224 | tf_op jit(solution)/shard_map/concatenate | solution.py:96
  38.0 2.1 %fusion.44 = (f32[4,128]{1,0:T(4,128)S(1)}, f32[4,128,2176]{2,1,0:T(8,128)S(1)}) fusion(bf16[128,4,64]{0,2,1:T(8,128)(2,1)S(1)} %bitcast.66, bf16[2176,4,64]{0,2,1:T(8,128)(2,1)} %bitcast.59, pred[2176]{0:T(1024)(128)(4,1)S(1)} %concatenate.31), kind=kOutput, calls=%fused_computation.61 | convolution fusion | flops 145948160 | bytes 5640320 | tf_op jit(solution)/shard_map/qhd,khd->hqk/dot_general | solution.py:42
  40.2 0.0 copy-start.3
  40.2 0.7 fusion.2
  40.9 0.5 copy-done.3
  41.4 0.0 copy-start.6
  41.4 0.0 copy-start.7
  41.4 0.0 copy-start.1
  41.5 1.0 fusion.33
  42.5 0.0 copy-done
  42.5 1.0 convolution_convert_fusion.1
  43.5 0.0 all-reduce.4.cloned.1.call-update
  43.5 0.0 all-reduce.6.cloned.1.call-start
  43.5 0.0 copy-done.6
  43.5 0.0 copy-done.7
  43.6 0.0 copy-done.8
  43.6 0.0 copy-done.9
  43.6 62.3 %all-reduce.4.cloned.1.call-done = bf16[128,1024]{1,0:T(8,128)(2,1)} async-done(((bf16[128,1024]{1,0:T(8,128)(2,1)}), bf16[128,1024]{1,0:T(8,128)(2,1)}) %all-reduce.4.cloned.1.call-update) | async-done | bytes 262160 | tf_op jit(solution)/shard_map/psum | solution.py:107
  105.9 0.0 copy-done.1
  105.9 1.1 fusion.36
  107.1 1.2 multiply_reduce_fusion.1
  108.2 1.2 fusion.38
  109.4 1.3 fusion.29
  110.7 1.3 fusion.28
  112.0 1.3 fusion.27
  113.3 1.1 pad_maximum_fusion.3
  114.4 1.7 copy.27
  116.0 0.1 copy.26
  116.1 1.1 pad_maximum_fusion.2
  117.2 2.3 %copy.25 = bf16[2176,256]{0,1:T(8,128)(2,1)} copy(bf16[2176,256]{1,0:T(8,128)(2,1)} %pad_maximum_fusion.2) | data formatting | bytes 2228224 | tf_op jit(solution)/shard_map/concatenate | solution.py:96
  119.6 0.9 fusion.45
  120.4 0.0 copy-start.2
  120.4 0.7 fusion.4
  121.2 0.5 copy-done.2
  121.7 1.0 fusion.30
  122.7 1.0 convolution_convert_fusion
  123.7 0.0 all-reduce.6.cloned.1.call-update
  123.7 52.7 %all-reduce.6.cloned.1.call-done = bf16[128,1024]{1,0:T(8,128)(2,1)} async-done(((bf16[128,1024]{1,0:T(8,128)(2,1)}), bf16[128,1024]{1,0:T(8,128)(2,1)}) %all-reduce.6.cloned.1.call-update) | async-done | bytes 262160 | tf_op jit(solution)/shard_map/psum | solution.py:107
  176.4 1.1 fusion.37
  177.5 1.2 multiply_reduce_fusion
  178.7 1.8 fusion.39
  (11 shorter events, 0.1 us)
Async XLA Ops:
  6.5 36.0 %copy-start = (bf16[256,1024]{1,0:T(8,128)(2,1)S(1)}, bf16[256,1024]{1,0:T(8,128)(2,1)}, u32[]{:S(2)}) copy-start(bf16[256,1024]{1,0:T(8,128)(2,1)} %param.26) | copy-start | bytes 1572868
  6.5 22.3 %copy-start.4 = (bf16[1,1024,256]{2,1,0:T(8,128)(2,1)S(1)}, bf16[1,1024,256]{2,1,0:T(8,128)(2,1)}, u32[]{:S(2)}) copy-start(bf16[1,1024,256]{2,1,0:T(8,128)(2,1)} %param.19) | copy-start | bytes 1572868
  6.5 99.4 %all-reduce.4.cloned.1.call-start = ((), (), s32[]{:S(2)}) async-start(), calls=%async_computation | async-start | bytes 524288 | tf_op jit(solution)/shard_map/psum | solution.py:107
  6.5 14.8 %collective-permute-start = (bf16[1024,256]{1,0:T(8,128)(2,1)}, bf16[1024,256]{1,0:T(8,128)(2,1)S(1)}, u32[]{:S(2)}, u32[]{:S(2)}) collective-permute-start(bf16[1024,256]{1,0:T(8,128)(2,1)} %bitcast.62), channel_id=1, source_target_pairs={{0,4},{4,0},{8,12},{12,8},{16,20},{20,16},{24,28},{28,24},{32,36},... | collective-permute-start | bytes 1572872 | tf_op jit(solution)/shard_map/ppermute | solution.py:14
  10.6 18.2 %collective-permute-start.1 = (bf16[1024,256]{1,0:T(8,128)(2,1)}, bf16[1024,256]{1,0:T(8,128)(2,1)}, u32[]{:S(2)}, u32[]{:S(2)}) collective-permute-start(bf16[1024,256]{1,0:T(8,128)(2,1)} %bitcast.64), channel_id=1, source_target_pairs={{0,4},{4,0},{8,12},{12,8},{16,20},{20,16},{24,28},{28,24},{32,36},... | collective-permute-start | bytes 1572872 | tf_op jit(solution)/shard_map/ppermute | solution.py:14
  21.3 0.8 copy-start.5
  40.2 1.3 copy-start.3
  41.4 2.1 %copy-start.6 = (bf16[1024]{0:T(1024)(128)(2,1)S(1)}, bf16[1024]{0:T(1024)(128)(2,1)}, u32[]{:S(2)}) copy-start(bf16[1024]{0:T(1024)(128)(2,1)} %param.27) | copy-start | bytes 6148
  41.4 2.1 %copy-start.7 = (bf16[1024]{0:T(1024)(128)(2,1)S(1)}, bf16[1024]{0:T(1024)(128)(2,1)}, u32[]{:S(2)}) copy-start(bf16[1024]{0:T(1024)(128)(2,1)} %param.28) | copy-start | bytes 6148
  41.4 2.1 %copy-start.8 = (bf16[1024]{0:T(1024)(128)(2,1)S(1)}, bf16[1024]{0:T(1024)(128)(2,1)}, u32[]{:S(2)}) copy-start(bf16[1024]{0:T(1024)(128)(2,1)} %param.29) | copy-start | bytes 6148
  41.4 2.2 %copy-start.9 = (s32[1,128]{1,0:T(1,128)S(1)}, s32[1,128]{1,0:T(1,128)}, u32[]{:S(2)}) copy-start(s32[1,128]{1,0:T(1,128)} %param.16) | copy-start | bytes 1540
  41.4 64.5 %copy-start.1 = (bf16[1,128,1024]{2,1,0:T(8,128)(2,1)S(1)}, bf16[1,128,1024]{2,1,0:T(8,128)(2,1)}, u32[]{:S(2)}) copy-start(bf16[1,128,1024]{2,1,0:T(8,128)(2,1)} %param.15) | copy-start | bytes 786436
  43.5 132.9 %all-reduce.6.cloned.1.call-start = ((), (), s32[]{:S(2)}) async-start(), calls=%async_computation.1 | async-start | bytes 524288 | tf_op jit(solution)/shard_map/psum | solution.py:107
  120.4 1.3 copy-start.2
Sparse Core Ops, SparseCore 0:
  43.6 62.2 all-reduce.3
  123.8 52.5 all-reduce.5
where the time goes:
time: 188 us; the launch traced here: 187 us
  waiting for transfers between devices  122 us (65%)
  other arithmetic  18.4 us (10%)
  matrix products  14.9 us (8%)
  between operations  14.3 us (8%)
  local copies, waits for them, and re-layouts  12 us (6%)
  starting transfers between devices  6.04 us (3%)
    psum x2, waiting for transfers between devices, one_pass(): lax.psum(partial_value.astype(jnp.bfloat16), 'tensor').astype(jnp.float32)  115 us
    dot_general x6, matrix products, project(): jnp.dot(inputs, weight, preferred_element_type=jnp.float32)  7.91 us
    ppermute x2, waiting for transfers between devices, swapped(): lax.ppermute(array, axis, [(i, i ^ 1 << apart) for i in range(lax.axis_si...  6.68 us
    ppermute x2, starting transfers between devices, swapped(): lax.ppermute(array, axis, [(i, i ^ 1 << apart) for i in range(lax.axis_si...  5.99 us
    concatenate x2, local copies, waits for them, and re-layouts, one_pass(): jnp.concatenate([pool_v, new_v], 0)  4.7 us
    concatenate x2, local copies, waits for them, and re-layouts, one_pass(): jnp.concatenate([pool_k, new_k], 0)  3.99 us
  transfers between devices with their start and end apart: 4, of which 3 were waited for; matrix products, arithmetic and copies ran while one was open for 4% of the time, Pallas kernels for 0%

commit v1 on v0

v1 whole, which is shorter than its diff:
```python
import jax
import jax.numpy as jnp
from jax import lax
from jax.experimental import pallas as pl
from jax.experimental.pallas import tpu as pltpu
from jax.sharding import PartitionSpec as P

HD = 64
NEG = -1e30
EPS = 1e-05
F32 = jnp.float32
BF16 = jnp.bfloat16
MIB = 1 << 20


def mm(left, right):
    return jnp.dot(left, right, preferred_element_type=F32)


def mm_t(left, right):
    return lax.dot_general(left, right, (((1,), (1,)), ((), ())), preferred_element_type=F32)


def project(rows, w_ref, b_ref):
    return (mm(rows, w_ref[...]) + b_ref[...].astype(F32)).astype(BF16)


def stack_heads(queries):
    scaled = queries * BF16(HD**-0.5)
    head_of = lax.broadcasted_iota(jnp.int32, scaled.shape, 1) // HD
    heads = scaled.shape[1] // HD
    return jnp.concatenate(
        [jnp.where(head_of == head, scaled, jnp.zeros_like(scaled)) for head in range(heads)], 0
    )


def unstack_heads(stacked, rows):
    heads = stacked.shape[0] // rows
    head_of = lax.broadcasted_iota(jnp.int32, (rows, stacked.shape[1]), 1) // HD
    merged = stacked[:rows]
    for head in range(1, heads):
        merged = jnp.where(head_of == head, stacked[head * rows : (head + 1) * rows], merged)
    return merged


def bias_row(count, low, high):
    place = lax.broadcasted_iota(jnp.int32, (1, count), 1)
    return jnp.where((place >= low) & (place < high), F32(0), F32(NEG))


def layer_norm(summed, gain_ref, shift_ref):
    centre = summed - jnp.mean(summed, -1, keepdims=True)
    spread = jnp.mean(centre * centre, -1, keepdims=True)
    return (
        centre * lax.rsqrt(spread + EPS) * gain_ref[...].astype(F32) + shift_ref[...].astype(F32)
    ).astype(BF16)


def own_kernel(
    lim_ref, x_ref, wq_ref, wk_ref, wv_ref, bq_ref, bk_ref, bv_ref, k_ref, v_ref,
    q_ref, acc_ref, max_ref, sum_ref,
):
    rows = x_ref[...]
    stacked = stack_heads(project(rows, wq_ref, bq_ref))
    q_ref[...] = stacked
    new_k = project(rows, wk_ref, bk_ref)
    new_v = project(rows, wv_ref, bv_ref)
    s_own = mm_t(stacked, k_ref[...]) + bias_row(k_ref.shape[0], lim_ref[0], lim_ref[1])
    s_new = mm_t(stacked, new_k)
    top = jnp.maximum(jnp.max(s_own, -1, keepdims=True), jnp.max(s_new, -1, keepdims=True))
    e_own = jnp.exp(s_own - top)
    e_new = jnp.exp(s_new - top)
    total = jnp.sum(e_own, -1, keepdims=True) + jnp.sum(e_new, -1, keepdims=True)
    acc_ref[...] = mm(e_own.astype(BF16), v_ref[...]) + mm(e_new.astype(BF16), new_v)
    max_ref[...] = jnp.broadcast_to(top, max_ref.shape)
    sum_ref[...] = jnp.broadcast_to(total, sum_ref.shape)


def peer_score_kernel(lim_ref, q_ref, k_ref, acc_ref, max_ref, sum_ref, e_ref, out_ref, total_ref):
    scores = mm_t(q_ref[...], k_ref[...]) + bias_row(k_ref.shape[0], lim_ref[2], lim_ref[3])
    before = max_ref[:, :1]
    top = jnp.maximum(before, jnp.max(scores, -1, keepdims=True))
    expo = jnp.exp(scores - top)
    shrink = jnp.exp(before - top)
    total = sum_ref[:, :1] * shrink + jnp.sum(expo, -1, keepdims=True)
    e_ref[...] = expo.astype(BF16)
    out_ref[...] = acc_ref[...] * shrink
    total_ref[...] = jnp.broadcast_to(total, total_ref.shape)


def peer_value_kernel(e_ref, v_ref, acc_ref, total_ref, att_ref):
    summed = acc_ref[...] + mm(e_ref[...], v_ref[...])
    att_ref[...] = unstack_heads(summed / total_ref[:, :1], att_ref.shape[0]).astype(BF16)


def out_project(lim_ref, att_ref, wo_refs, bo_ref, rows, gain_ref, shift_ref):
    summed = bo_ref[...].astype(F32) + rows.astype(F32)
    me = lim_ref[4]
    for apart, wo_ref in enumerate(wo_refs):
        summed += mm(att_ref[me ^ apart], wo_ref[...])
    return layer_norm(summed, gain_ref, shift_ref)


def second_kernel(
    lim_ref, att_ref, wo0, wo1, wo2, wo3, bo_ref, gain_ref, shift_ref, x_ref, mask_ref,
    wq_ref, wk_ref, wv_ref, bq_ref, bk_ref, bv_ref, k_ref, v_ref, pk_ref, pv_ref,
    second_ref, att_out_ref,
):
    block = x_ref[...]
    first = out_project(lim_ref, att_ref, (wo0, wo1, wo2, wo3), bo_ref, block, gain_ref, shift_ref)
    rows = jnp.where(mask_ref[:, :1] == 1, first, block)
    second_ref[...] = rows
    stacked = stack_heads(project(rows, wq_ref, bq_ref))
    new_k = project(rows, wk_ref, bk_ref)
    new_v = project(rows, wv_ref, bv_ref)
    count = k_ref.shape[0]
    s_own = mm_t(stacked, k_ref[...]) + bias_row(count, lim_ref[0], lim_ref[1])
    s_peer = mm_t(stacked, pk_ref[...]) + bias_row(count, lim_ref[2], lim_ref[3])
    s_new = mm_t(stacked, new_k)
    top = jnp.maximum(
        jnp.maximum(jnp.max(s_own, -1, keepdims=True), jnp.max(s_peer, -1, keepdims=True)),
        jnp.max(s_new, -1, keepdims=True),
    )
    e_own = jnp.exp(s_own - top)
    e_peer = jnp.exp(s_peer - top)
    e_new = jnp.exp(s_new - top)
    total = (
        jnp.sum(e_own, -1, keepdims=True)
        + jnp.sum(e_peer, -1, keepdims=True)
        + jnp.sum(e_new, -1, keepdims=True)
    )
    summed = (
        mm(e_own.astype(BF16), v_ref[...])
        + mm(e_peer.astype(BF16), pv_ref[...])
        + mm(e_new.astype(BF16), new_v)
    )
    att_out_ref[...] = unstack_heads(summed / total, block.shape[0]).astype(BF16)


def last_kernel(lim_ref, att_ref, wo0, wo1, wo2, wo3, bo_ref, gain_ref, shift_ref, x_ref, out_ref):
    out_ref[...] = out_project(
        lim_ref, att_ref, (wo0, wo1, wo2, wo3), bo_ref, x_ref[...], gain_ref, shift_ref
    )


def call(kernel, name, outs, *args, flops=1 << 28, limit=24):
    specs = [pl.BlockSpec(memory_space=pltpu.SMEM) if arg.ndim == 1 else pl.BlockSpec(memory_space=pltpu.VMEM) for arg in args]
    return pl.pallas_call(
        kernel,
        name=name,
        out_shape=outs,
        in_specs=specs,
        out_specs=jax.tree.map(lambda _: pl.BlockSpec(memory_space=pltpu.VMEM), outs),
        compiler_params=pltpu.CompilerParams(vmem_limit_bytes=limit * MIB),
        cost_estimate=pl.CostEstimate(flops=flops, bytes_accessed=1 << 22, transcendentals=1 << 19),
    )(*args)


def moved(array, axis, apart):
    return lax.ppermute(array, axis, [(i, i ^ apart) for i in range(lax.axis_size(axis))])


def body(
    block, mask, cache_len, cache_k, cache_v, w_q, b_q, w_k, b_k, w_v, b_v, w_o, b_o, ln_gain, ln_shift
):
    rows = block[0]
    own_k, own_v = cache_k[0], cache_v[0]
    slab, width = own_k.shape
    count = rows.shape[0]
    stack = count * (width // HD)
    group = lax.axis_index("group")
    parity = group % 2
    length = cache_len[group]
    even = parity == 0
    lims = jnp.stack(
        [
            jnp.where(even, 0, slab - length),
            jnp.where(even, length, slab),
            jnp.where(even, 0, 2 * slab - length),
            jnp.where(even, length - slab, slab),
            lax.axis_index("tensor"),
        ]
    ).astype(jnp.int32)
    row = lambda vector: vector.reshape(1, -1)
    b_q, b_k, b_v, b_o, ln_gain, ln_shift = map(row, (b_q, b_k, b_v, b_o, ln_gain, ln_shift))
    mask_cols = jnp.broadcast_to(mask[0][:, None], (count, 128))

    peer_k = moved(own_k, "group", 1)
    peer_v = moved(own_v, "group", 1)
    wo_late, lims = lax.optimization_barrier((w_o, lims))
    wo2 = moved(wo_late, "tensor", 2)
    shape = jax.ShapeDtypeStruct
    stats = shape((stack, 128), F32)
    q_stack, acc, top, total = call(
        own_kernel, "own",
        (shape((stack, width), BF16), shape((stack, width), F32), stats, stats),
        lims, rows, w_q, w_k, w_v, b_q, b_k, b_v, own_k, own_v,
    )
    wo_later, acc = lax.optimization_barrier((w_o, acc))
    wo1 = moved(wo_later, "tensor", 1)
    wo2, acc = lax.optimization_barrier((wo2, acc))
    wo3 = moved(wo2, "tensor", 1)
    wo = (w_o, wo1, wo2, wo3)
    expo, acc, total = call(
        peer_score_kernel, "peer_score",
        (shape((stack, slab), BF16), shape((stack, width), F32), stats),
        lims, q_stack, peer_k, acc, top, total,
    )
    att = call(peer_value_kernel, "peer_value", shape((count, width), BF16), expo, peer_v, acc, total)
    att = lax.all_gather(att, "tensor")
    second, att = call(
        second_kernel, "second",
        (shape(rows.shape, BF16), shape((count, width), BF16)),
        lims, att, *wo, b_o, ln_gain, ln_shift, rows, mask_cols,
        w_q, w_k, w_v, b_q, b_k, b_v, own_k, own_v, peer_k, peer_v,
    )
    att = lax.all_gather(att, "tensor")
    out = call(
        last_kernel, "last", shape(rows.shape, BF16),
        lims, att, *wo, b_o, ln_gain, ln_shift, second,
    )
    return out[None]


def solution(mesh):
    return jax.shard_map(
        body,
        mesh=mesh,
        in_specs=(
            P("group", None, None),
            P("group", None),
            P(),
            P("group", None, "tensor"),
            P("group", None, "tensor"),
            P(None, "tensor"),
            P("tensor"),
            P(None, "tensor"),
            P("tensor"),
            P(None, "tensor"),
            P("tensor"),
            P("tensor", None),
            P(),
            P(),
            P(),
        ),
        out_specs=P("group", None, None),
        check_vma=False,
    )
```

time: 188 us -> 56 us (0.30)
  waiting for transfers between devices: 122 us -> 0.01 us
  other arithmetic: 18.4 us -> 0 us
  matrix products: 14.9 us -> 0 us
  blocking collectives: 0 us -> 12.6 us
  starting transfers between devices: 6.04 us -> 18.5 us
  Pallas kernels: 0 us -> 11.8 us
  between operations: 14.3 us -> 2.89 us
  local copies, waits for them, and re-layouts: 12 us -> 9.59 us
    psum x2 -> x0, waiting for transfers between devices: 115 us -> none  [one_pass(): lax.psum(partial_value.astype(jnp.bfloat16), 'tensor').astype(jnp.float32)]
    dot_general x12 -> x0, matrix products: 14.9 us -> none  [the longest x6 7.91 us: project(): jnp.dot(inputs, weight, preferred_element_type=jnp.float32)]
    all_gather x0 -> x2, blocking collectives: none -> 12.6 us  [body(): att = lax.all_gather(att, 'tensor')]
    ppermute x2 -> x5, starting transfers between devices: 5.99 us -> 18.5 us  [moved(): lax.ppermute(array, axis, [(i, i ^ apart) for i in range(lax.axis_size(ax...]
    pallas_call x0 -> x5, Pallas kernels: none -> 11.8 us  [call(): pl.pallas_call(kernel, name=name, out_shape=outs, in_specs=specs, out_spe...]
    concatenate x5 -> x0, local copies, waits for them, and re-layouts: 8.7 us -> none  [the longest x2 4.7 us: one_pass(): jnp.concatenate([pool_v, new_v], 0)]
    unnamed x20 -> x42, local copies, waits for them, and re-layouts: 1.82 us -> 8.83 us
    ppermute x2 -> x5, waiting for transfers between devices: 6.68 us -> 0.01 us  [moved(): lax.ppermute(array, axis, [(i, i ^ apart) for i in range(lax.axis_size(ax...]
  transfers between devices with their start and end apart: 4 -> 5, of which waited for: 3 -> 0; matrix products, arithmetic and copies ran while one was open for 4% -> 0% of each run, Pallas kernels for 0% -> 10%
where the time goes in v1:
time: 56 us; the launch traced here: 55.4 us
  starting transfers between devices  18.5 us (33%)
  blocking collectives  12.6 us (22%)
  Pallas kernels  11.8 us (21%)
  local copies, waits for them, and re-layouts  9.59 us (17%)
  between operations  2.89 us (5%)
    ppermute x5, starting transfers between devices, moved(): lax.ppermute(array, axis, [(i, i ^ apart) for i in range(lax.axis_size(ax...  18.5 us
    all_gather x2, blocking collectives, body(): att = lax.all_gather(att, 'tensor')  12.6 us
    pallas_call x5, Pallas kernels, call(): pl.pallas_call(kernel, name=name, out_shape=outs, in_specs=specs, out_spe...  11.8 us
    unnamed x42, local copies, waits for them, and re-layouts  8.83 us
  transfers between devices with their start and end apart: 5, of which 0 were waited for; matrix products, arithmetic and copies ran while one was open for 0% of the time, Pallas kernels for 10%

profile of v1, /device:TPU:1, one launch (start us, length us, event | category | flops | bytes accessed | tf_op | source)
XLA Modules:
  0.0 55.4 jit_solution(7657201456835376618)
XLA Ops:
  0.0 0.0 copy-start.17
  0.0 0.7 %copy-done.17 = s32[128]{0:T(128)S(1)} copy-done((s32[128]{0:T(128)S(1)}, s32[128]{0:T(128)}, u32[]{:S(2)}) %copy-start.17) | copy-done | bytes 536
  0.7 0.6 %dynamic_slice.3 = s32[1]{0:T(128)} dynamic-slice(s32[128]{0:T(128)S(1)} %copy-done.17, s32[]{:T(128)S(6)} %select_n.25), dynamic_slice_sizes={1} | dynamic-slice | bytes 12 | tf_op jit(solution)/shard_map/dynamic_slice | solution.py:173
  3.8 0.1 stack.23.lim_ref
  3.9 4.0 %collective-permute-start.1 = (bf16[256,1024]{1,0:T(8,128)(2,1)}, bf16[256,1024]{1,0:T(8,128)(2,1)S(1)}, u32[]{:S(2)}, u32[]{:S(2)}) collective-permute-start(bf16[256,1024]{1,0:T(8,128)(2,1)} %wo0.3), channel_id=1, source_target_pairs={{0,2},{1,3},{2,0},{3,1},{4,6},{5,7},{6,4},{7,5},{8,10},{9,11},{10,... | collective-permute-start | bytes 1572872 | tf_op jit(solution)/shard_map/ppermute | solution.py:160
  8.0 0.0 copy-start.18
  8.0 3.1 %collective-permute-start = (bf16[1024,256]{1,0:T(8,128)(2,1)}, bf16[1024,256]{1,0:T(8,128)(2,1)S(1)}, u32[]{:S(2)}, u32[]{:S(2)}) collective-permute-start(bf16[1024,256]{1,0:T(8,128)(2,1)} %bitcast.13), channel_id=1, source_target_pairs={{0,4},{4,0},{8,12},{12,8},{16,20},{20,16},{24,28},{28,24},{32,36},... | collective-permute-start | bytes 1572872 | tf_op jit(solution)/shard_map/ppermute | solution.py:160
  11.1 0.0 copy-start.19
  11.1 2.2 %collective-permute-start.2 = (bf16[1024,256]{1,0:T(8,128)(2,1)}, bf16[1024,256]{1,0:T(8,128)(2,1)S(1)}, u32[]{:S(2)}, u32[]{:S(2)}) collective-permute-start(bf16[1024,256]{1,0:T(8,128)(2,1)} %bitcast.16), channel_id=1, source_target_pairs={{0,4},{4,0},{8,12},{12,8},{16,20},{20,16},{24,28},{28,24},{32,36},... | collective-permute-start | bytes 1572872 | tf_op jit(solution)/shard_map/ppermute | solution.py:160
  13.3 0.0 copy-done.18
  13.3 0.0 copy-done.19
  13.3 0.0 copy-start.20
  13.3 0.6 %copy-done.20 = bf16[256]{0:T(256)(128)(2,1)S(1)} copy-done((bf16[256]{0:T(256)(128)(2,1)S(1)}, bf16[256]{0:T(256)(128)(2,1)}, u32[]{:S(2)}) %copy-start.20) | copy-done | bytes 536
  14.0 0.0 copy-start
  14.0 1.0 %copy-done = bf16[1024,256]{1,0:T(8,128)(2,1)S(1)} copy-done((bf16[1024,256]{1,0:T(8,128)(2,1)S(1)}, bf16[1024,256]{1,0:T(8,128)(2,1)}, u32[]{:S(2)}) %copy-start) | copy-done | bytes 524312
  15.0 0.0 copy-start.2
  15.0 1.0 %copy-done.2 = bf16[1024,256]{1,0:T(8,128)(2,1)S(1)} copy-done((bf16[1024,256]{1,0:T(8,128)(2,1)S(1)}, bf16[1024,256]{1,0:T(8,128)(2,1)}, u32[]{:S(2)}) %copy-start.2) | copy-done | bytes 524312
  16.1 0.0 copy-start.4
  16.1 1.0 %copy-done.4 = bf16[1024,256]{1,0:T(8,128)(2,1)S(1)} copy-done((bf16[1024,256]{1,0:T(8,128)(2,1)S(1)}, bf16[1024,256]{1,0:T(8,128)(2,1)}, u32[]{:S(2)}) %copy-start.4) | copy-done | bytes 524312
  17.1 0.0 copy-start.6
  17.1 1.0 %copy-done.6 = bf16[1,1024,256]{2,1,0:T(8,128)(2,1)S(1)} copy-done((bf16[1,1024,256]{2,1,0:T(8,128)(2,1)S(1)}, bf16[1,1024,256]{2,1,0:T(8,128)(2,1)}, u32[]{:S(2)}) %copy-start.6) | copy-done | bytes 524312
  18.1 0.0 copy-start.8
  18.1 1.0 %copy-done.8 = bf16[1,1024,256]{2,1,0:T(8,128)(2,1)S(1)} copy-done((bf16[1,1024,256]{2,1,0:T(8,128)(2,1)S(1)}, bf16[1,1024,256]{2,1,0:T(8,128)(2,1)}, u32[]{:S(2)}) %copy-start.8) | copy-done | bytes 524312
  19.2 0.0 copy-start.11
  19.2 0.9 %copy-done.11 = bf16[1,128,1024]{2,1,0:T(8,128)(2,1)S(1)} copy-done((bf16[1,128,1024]{2,1,0:T(8,128)(2,1)S(1)}, bf16[1,128,1024]{2,1,0:T(8,128)(2,1)}, u32[]{:S(2)}) %copy-start.11) | copy-done | bytes 262168
  20.1 0.0 copy-start.10
  20.1 0.0 copy-start.13
  20.1 2.5 %own.1 = (bf16[512,256]{1,0:T(8,128)(2,1)S(1)}, f32[512,256]{1,0:T(8,128)S(1)}, f32[512,128]{1,0:T(8,128)S(1)}, f32[512,128]{1,0:T(8,128)S(1)}) custom-call(s32[5]{0:T(128)S(1)} %stack.23.lim_ref, bf16[128,1024]{1,0:T(8,128)(2,1)S(1)} %bitcast.19, bf16[1024,256]{1,0:T(8,128)(2,1)S(1)} %copy-done, bf16[1024,256]{1,0:T(8,128)(2,1)S(1)} %copy-done.2, ...), custom_call_target="tpu_custom_call" | custom-call | flops 268435456 | bytes 4194304 | tf_op jit(solution)/shard_map/own/pallas_call | solution.py:148
  22.7 0.0 copy-done.10
  22.7 0.0 copy-start.14
  22.7 7.2 %collective-permute-start.3 = (bf16[256,1024]{1,0:T(8,128)(2,1)S(1)}, bf16[256,1024]{1,0:T(8,128)(2,1)S(1)}, u32[]{:S(2)}, u32[]{:S(2)}) collective-permute-start(bf16[256,1024]{1,0:T(8,128)(2,1)S(1)} %copy-done.10), channel_id=1, source_target_pairs={{0,1},{1,0},{2,3},{3,2},{4,5},{5,4},{6,7},{7,6},{8,9},{9,8},{10,11... | collective-permute-start | bytes 1572872 | tf_op jit(solution)/shard_map/ppermute | solution.py:160
  29.9 0.0 collective-permute-done.1.wo2
  30.0 1.9 %collective-permute-start.4 = (bf16[256,1024]{1,0:T(8,128)(2,1)S(1)}, bf16[256,1024]{1,0:T(8,128)(2,1)S(1)}, u32[]{:S(2)}, u32[]{:S(2)}) collective-permute-start(bf16[256,1024]{1,0:T(8,128)(2,1)S(1)} %collective-permute-done.1.wo2), channel_id=1, source_target_pairs={{0,1},{1,0},{2,3},{3,2},{4,5},{5,4},{6,7},{7,6},{8,9},{9,8},{10,11... | collective-permute-start | bytes 1572872 | tf_op jit(solution)/shard_map/ppermute | solution.py:160
  31.9 0.0 copy-done.13
  31.9 0.0 copy-done.14
  31.9 0.0 copy-start.15
  31.9 0.7 %copy-done.15 = bf16[1024]{0:T(1024)(128)(2,1)S(1)} copy-done((bf16[1024]{0:T(1024)(128)(2,1)S(1)}, bf16[1024]{0:T(1024)(128)(2,1)}, u32[]{:S(2)}) %copy-start.15) | copy-done | bytes 2072
  32.6 0.0 collective-permute-done.k_ref.pk_ref
  32.6 0.0 copy-start.12
  32.6 2.4 %peer_score.1 = (bf16[512,1024]{1,0:T(8,128)(2,1)S(1)}, f32[512,256]{1,0:T(8,128)S(1)}, f32[512,128]{1,0:T(8,128)S(1)}) custom-call(s32[5]{0:T(128)S(1)} %stack.23.lim_ref, bf16[512,256]{1,0:T(8,128)(2,1)S(1)} %get-tuple-element.21.q_ref, bf16[1024,256]{1,0:T(8,128)(2,1)S(1)} %collective-permute-done.k_ref.pk_ref, f32[512,256]{1,0:T(8,128)S(1)} %get-tuple-element.25.acc_ref, ...), custom_call_target="tpu_custom_call" | custom-call | flops 268435456 | bytes 4194304 | tf_op jit(solution)/shard_map/peer_score/pallas_call | solution.py:148
  35.0 0.0 collective-permute-done.2.v_ref.pv_ref
  35.0 0.0 copy-start.1
  35.0 0.0 copy-start.3
  35.0 0.0 copy-start.5
  35.0 0.0 copy-start.7
  35.0 0.0 copy-start.9
  35.1 0.4 peer_value.1
  35.5 6.7 %all-gather = bf16[512,256]{1,0:T(8,128)(2,1)S(1)} all-gather(bf16[128,256]{1,0:T(8,128)(2,1)S(1)} %peer_value.1), channel_id=2, replica_groups=mesh['group'=128,'tensor'=4] {'tensor'}, dimensions={0}, use_global_device_ids=true | all-gather | bytes 327680 | tf_op jit(solution)/shard_map/all_gather | solution.py:210
  42.2 0.0 collective-permute-done.3.wo1
  42.3 0.0 collective-permute-done.4.wo3
  42.3 0.0 copy-start.16
  42.3 0.7 %copy-done.16 = s32[1,128]{1,0:T(1,128)S(1)} copy-done((s32[1,128]{1,0:T(1,128)S(1)}, s32[1,128]{1,0:T(1,128)}, u32[]{:S(2)}) %copy-start.16) | copy-done | bytes 536
  42.9 0.1 broadcast_in_dim.11.mask_ref
  43.0 0.0 copy-done.12
  43.0 0.0 copy-done.1
  43.0 0.0 copy-done.3
  43.0 0.0 copy-done.5
  43.0 0.0 copy-done.7
  43.0 0.0 copy-done.9
  43.0 4.5 %second.1 = (bf16[128,1024]{1,0:T(8,128)(2,1)S(1)}, bf16[128,256]{1,0:T(8,128)(2,1)S(1)}) custom-call(s32[5]{0:T(128)S(1)} %stack.23.lim_ref, bf16[4,128,256]{2,1,0:T(8,128)(2,1)S(1)} %bitcast.21, bf16[256,1024]{1,0:T(8,128)(2,1)S(1)} %copy-done.10, bf16[256,1024]{1,0:T(8,128)(2,1)S(1)} %collective-permute-done.3.wo1, ...), custom_call_target="tpu_custom_call" | custom-call | flops 268435456 | bytes 4194304 | tf_op jit(solution)/shard_map/second/pallas_call | solution.py:148
  47.6 5.9 %all-gather.1 = bf16[512,256]{1,0:T(8,128)(2,1)S(1)} all-gather(bf16[128,256]{1,0:T(8,128)(2,1)S(1)} %get-tuple-element.33), channel_id=3, replica_groups=mesh['group'=128,'tensor'=4] {'tensor'}, dimensions={0}, use_global_device_ids=true | all-gather | bytes 327680 | tf_op jit(solution)/shard_map/all_gather | solution.py:217
  53.5 1.9 %last.1 = bf16[128,1024]{1,0:T(8,128)(2,1)} custom-call(s32[5]{0:T(128)S(1)} %stack.23.lim_ref, bf16[4,128,256]{2,1,0:T(8,128)(2,1)S(1)} %bitcast.22, bf16[256,1024]{1,0:T(8,128)(2,1)S(1)} %copy-done.10, bf16[256,1024]{1,0:T(8,128)(2,1)S(1)} %collective-permute-done.3.wo1, bf16[256,1024]{1,0:T(8,128)(2,1)S(1)} %collective-permute-done.1.wo2, ...), custom_call_target="tpu_custom_call" | custom-call | flops 268435456 | bytes 4194304 | tf_op jit(solution)/shard_map/last/pallas_call | solution.py:148
  (6 shorter events, 0.0 us)
Async XLA Ops:
  0.0 0.7 %copy-start.17 = (s32[128]{0:T(128)S(1)}, s32[128]{0:T(128)}, u32[]{:S(2)}) copy-start(s32[128]{0:T(128)} %param.17) | copy-start | bytes 1540
  3.9 26.0 %collective-permute-start.1 = (bf16[256,1024]{1,0:T(8,128)(2,1)}, bf16[256,1024]{1,0:T(8,128)(2,1)S(1)}, u32[]{:S(2)}, u32[]{:S(2)}) collective-permute-start(bf16[256,1024]{1,0:T(8,128)(2,1)} %wo0.3), channel_id=1, source_target_pairs={{0,2},{1,3},{2,0},{3,1},{4,6},{5,7},{6,4},{7,5},{8,10},{9,11},{10,... | collective-permute-start | bytes 1572872 | tf_op jit(solution)/shard_map/ppermute | solution.py:160
  8.0 5.3 %copy-start.18 = (bf16[256]{0:T(256)(128)(2,1)S(1)}, bf16[256]{0:T(256)(128)(2,1)}, u32[]{:S(2)}) copy-start(bf16[256]{0:T(256)(128)(2,1)} %param.21) | copy-start | bytes 1540
  8.0 24.6 %collective-permute-start = (bf16[1024,256]{1,0:T(8,128)(2,1)}, bf16[1024,256]{1,0:T(8,128)(2,1)S(1)}, u32[]{:S(2)}, u32[]{:S(2)}) collective-permute-start(bf16[1024,256]{1,0:T(8,128)(2,1)} %bitcast.13), channel_id=1, source_target_pairs={{0,4},{4,0},{8,12},{12,8},{16,20},{20,16},{24,28},{28,24},{32,36},... | collective-permute-start | bytes 1572872 | tf_op jit(solution)/shard_map/ppermute | solution.py:160
  11.1 2.2 %copy-start.19 = (bf16[256]{0:T(256)(128)(2,1)S(1)}, bf16[256]{0:T(256)(128)(2,1)}, u32[]{:S(2)}) copy-start(bf16[256]{0:T(256)(128)(2,1)} %param.23) | copy-start | bytes 1540
  11.1 23.9 %collective-permute-start.2 = (bf16[1024,256]{1,0:T(8,128)(2,1)}, bf16[1024,256]{1,0:T(8,128)(2,1)S(1)}, u32[]{:S(2)}, u32[]{:S(2)}) collective-permute-start(bf16[1024,256]{1,0:T(8,128)(2,1)} %bitcast.16), channel_id=1, source_target_pairs={{0,4},{4,0},{8,12},{12,8},{16,20},{20,16},{24,28},{28,24},{32,36},... | collective-permute-start | bytes 1572872 | tf_op jit(solution)/shard_map/ppermute | solution.py:160
  13.3 0.7 %copy-start.20 = (bf16[256]{0:T(256)(128)(2,1)S(1)}, bf16[256]{0:T(256)(128)(2,1)}, u32[]{:S(2)}) copy-start(bf16[256]{0:T(256)(128)(2,1)} %param.25) | copy-start | bytes 1540
  14.0 1.0 %copy-start = (bf16[1024,256]{1,0:T(8,128)(2,1)S(1)}, bf16[1024,256]{1,0:T(8,128)(2,1)}, u32[]{:S(2)}) copy-start(bf16[1024,256]{1,0:T(8,128)(2,1)} %wq_ref.3) | copy-start | bytes 1572868
  15.0 1.0 %copy-start.2 = (bf16[1024,256]{1,0:T(8,128)(2,1)S(1)}, bf16[1024,256]{1,0:T(8,128)(2,1)}, u32[]{:S(2)}) copy-start(bf16[1024,256]{1,0:T(8,128)(2,1)} %wk_ref.3) | copy-start | bytes 1572868
  16.1 1.0 %copy-start.4 = (bf16[1024,256]{1,0:T(8,128)(2,1)S(1)}, bf16[1024,256]{1,0:T(8,128)(2,1)}, u32[]{:S(2)}) copy-start(bf16[1024,256]{1,0:T(8,128)(2,1)} %wv_ref.3) | copy-start | bytes 1572868
  17.1 1.0 %copy-start.6 = (bf16[1,1024,256]{2,1,0:T(8,128)(2,1)S(1)}, bf16[1,1024,256]{2,1,0:T(8,128)(2,1)}, u32[]{:S(2)}) copy-start(bf16[1,1024,256]{2,1,0:T(8,128)(2,1)} %param.18) | copy-start | bytes 1572868
  18.1 1.0 %copy-start.8 = (bf16[1,1024,256]{2,1,0:T(8,128)(2,1)S(1)}, bf16[1,1024,256]{2,1,0:T(8,128)(2,1)}, u32[]{:S(2)}) copy-start(bf16[1,1024,256]{2,1,0:T(8,128)(2,1)} %param.19) | copy-start | bytes 1572868
  19.2 0.9 %copy-start.11 = (bf16[1,128,1024]{2,1,0:T(8,128)(2,1)S(1)}, bf16[1,128,1024]{2,1,0:T(8,128)(2,1)}, u32[]{:S(2)}) copy-start(bf16[1,128,1024]{2,1,0:T(8,128)(2,1)} %param.15) | copy-start | bytes 786436
  20.1 2.5 %copy-start.10 = (bf16[256,1024]{1,0:T(8,128)(2,1)S(1)}, bf16[256,1024]{1,0:T(8,128)(2,1)}, u32[]{:S(2)}) copy-start(bf16[256,1024]{1,0:T(8,128)(2,1)} %wo0.3) | copy-start | bytes 1572868
  20.1 11.7 %copy-start.13 = (bf16[1024]{0:T(1024)(128)(2,1)S(1)}, bf16[1024]{0:T(1024)(128)(2,1)}, u32[]{:S(2)}) copy-start(bf16[1024]{0:T(1024)(128)(2,1)} %param.27) | copy-start | bytes 6148
  22.7 9.2 %copy-start.14 = (bf16[1024]{0:T(1024)(128)(2,1)S(1)}, bf16[1024]{0:T(1024)(128)(2,1)}, u32[]{:S(2)}) copy-start(bf16[1024]{0:T(1024)(128)(2,1)} %param.28) | copy-start | bytes 6148
  22.7 19.5 %collective-permute-start.3 = (bf16[256,1024]{1,0:T(8,128)(2,1)S(1)}, bf16[256,1024]{1,0:T(8,128)(2,1)S(1)}, u32[]{:S(2)}, u32[]{:S(2)}) collective-permute-start(bf16[256,1024]{1,0:T(8,128)(2,1)S(1)} %copy-done.10), channel_id=1, source_target_pairs={{0,1},{1,0},{2,3},{3,2},{4,5},{5,4},{6,7},{7,6},{8,9},{9,8},{10,11... | collective-permute-start | bytes 1572872 | tf_op jit(solution)/shard_map/ppermute | solution.py:160
  30.0 12.3 %collective-permute-start.4 = (bf16[256,1024]{1,0:T(8,128)(2,1)S(1)}, bf16[256,1024]{1,0:T(8,128)(2,1)S(1)}, u32[]{:S(2)}, u32[]{:S(2)}) collective-permute-start(bf16[256,1024]{1,0:T(8,128)(2,1)S(1)} %collective-permute-done.1.wo2), channel_id=1, source_target_pairs={{0,1},{1,0},{2,3},{3,2},{4,5},{5,4},{6,7},{7,6},{8,9},{9,8},{10,11... | collective-permute-start | bytes 1572872 | tf_op jit(solution)/shard_map/ppermute | solution.py:160
  31.9 0.7 %copy-start.15 = (bf16[1024]{0:T(1024)(128)(2,1)S(1)}, bf16[1024]{0:T(1024)(128)(2,1)}, u32[]{:S(2)}) copy-start(bf16[1024]{0:T(1024)(128)(2,1)} %param.29) | copy-start | bytes 6148
  32.6 10.4 %copy-start.12 = (bf16[1,128,1024]{2,1,0:T(8,128)(2,1)S(1)}, bf16[1,128,1024]{2,1,0:T(8,128)(2,1)}, u32[]{:S(2)}) copy-start(bf16[1,128,1024]{2,1,0:T(8,128)(2,1)} %param.15) | copy-start | bytes 786436
  35.0 8.0 %copy-start.1 = (bf16[1024,256]{1,0:T(8,128)(2,1)S(1)}, bf16[1024,256]{1,0:T(8,128)(2,1)}, u32[]{:S(2)}) copy-start(bf16[1024,256]{1,0:T(8,128)(2,1)} %wq_ref.3) | copy-start | bytes 1572868
  35.0 8.0 %copy-start.3 = (bf16[1024,256]{1,0:T(8,128)(2,1)S(1)}, bf16[1024,256]{1,0:T(8,128)(2,1)}, u32[]{:S(2)}) copy-start(bf16[1024,256]{1,0:T(8,128)(2,1)} %wk_ref.3) | copy-start | bytes 1572868
  35.0 8.0 %copy-start.5 = (bf16[1024,256]{1,0:T(8,128)(2,1)S(1)}, bf16[1024,256]{1,0:T(8,128)(2,1)}, u32[]{:S(2)}) copy-start(bf16[1024,256]{1,0:T(8,128)(2,1)} %wv_ref.3) | copy-start | bytes 1572868
  35.0 8.0 %copy-start.7 = (bf16[1,1024,256]{2,1,0:T(8,128)(2,1)S(1)}, bf16[1,1024,256]{2,1,0:T(8,128)(2,1)}, u32[]{:S(2)}) copy-start(bf16[1,1024,256]{2,1,0:T(8,128)(2,1)} %param.18) | copy-start | bytes 1572868
  35.0 8.0 %copy-start.9 = (bf16[1,1024,256]{2,1,0:T(8,128)(2,1)S(1)}, bf16[1,1024,256]{2,1,0:T(8,128)(2,1)}, u32[]{:S(2)}) copy-start(bf16[1,1024,256]{2,1,0:T(8,128)(2,1)} %param.19) | copy-start | bytes 1572868
  42.3 0.7 %copy-start.16 = (s32[1,128]{1,0:T(1,128)S(1)}, s32[1,128]{1,0:T(1,128)}, u32[]{:S(2)}) copy-start(s32[1,128]{1,0:T(1,128)} %param.16) | copy-start | bytes 1540

commit v2 on v1

v2 whole, which is shorter than its diff:
```python
import jax
import jax.numpy as jnp
from jax import lax
from jax.experimental import pallas as pl
from jax.experimental.pallas import tpu as pltpu
from jax.sharding import PartitionSpec as P

HD = 64
SHORTEST = 128
NEG = -1e30
EPS = 1e-05
F32 = jnp.float32
BF16 = jnp.bfloat16
MIB = 1 << 20
LOG2E = 1.4426950408889634
STEP = 16


def mm(left, right):
    return jnp.dot(left, right, preferred_element_type=F32)


def mm_t(left, right):
    return lax.dot_general(left, right, (((1,), (1,)), ((), ())), preferred_element_type=F32)


def project(rows, w_ref, b_ref):
    return (mm(rows, w_ref[...]) + b_ref[...].astype(F32)[None]).astype(BF16)


def stack_queries(rows, w_ref, b_ref):
    scaled = (
        (mm(rows, w_ref[...]) + b_ref[...].astype(F32)[None]) * F32(LOG2E * HD**-0.5)
    ).astype(BF16)
    head_of = lax.broadcasted_iota(jnp.int32, scaled.shape, 1) // HD
    heads = scaled.shape[1] // HD
    return jnp.concatenate(
        [jnp.where(head_of == head, scaled, jnp.zeros_like(scaled)) for head in range(heads)], 0
    )


def unstack_heads(stacked, rows):
    heads = stacked.shape[0] // rows
    head_of = lax.broadcasted_iota(jnp.int32, (rows, stacked.shape[1]), 1) // HD
    merged = stacked[:rows]
    for head in range(1, heads):
        merged = jnp.where(head_of == head, stacked[head * rows : (head + 1) * rows], merged)
    return merged


def own_span(len_ref, slab):
    group = lax.axis_index("group")
    length = len_ref[group]
    even = group % 2 == 0
    return jnp.where(even, 0, slab - length), jnp.where(even, length, slab)


def peer_span(len_ref, kept):
    group = lax.axis_index("group")
    beyond = len_ref[group] - (kept + SHORTEST)
    even = group % 2 == 0
    return jnp.where(even, 0, kept - beyond), jnp.where(even, beyond, kept)


def bias_row(count, span):
    low, high = span
    place = lax.broadcasted_iota(jnp.int32, (1, count), 1)
    return jnp.where((place >= low) & (place < high), F32(0), F32(NEG))


def column(row_ref):
    count = row_ref.shape[1]
    square = jnp.broadcast_to(row_ref[...], (count, count))
    across = lax.broadcasted_iota(jnp.int32, square.shape, 1)
    down = lax.broadcasted_iota(jnp.int32, square.shape, 0)
    return jnp.sum(jnp.where(across == down, square, 0), -1, keepdims=True)


def layer_norm(summed, norm_ref):
    centre = summed - jnp.mean(summed, -1, keepdims=True)
    spread = jnp.mean(centre * centre, -1, keepdims=True)
    return (
        centre * lax.rsqrt(spread + EPS) * norm_ref[1:2, :] + norm_ref[2:3, :]
    ).astype(BF16)


def own_kernel(
    len_ref, mask_ref, x_ref, wq_ref, wk_ref, wv_ref, bq_ref, bk_ref, bv_ref, k_ref, v_ref,
    bo_ref, gain_ref, shift_ref,
    q_ref, acc_ref, max_ref, sum_ref, picked_ref, norm_ref, bias_ref, kt_ref,
):
    slab = k_ref.shape[0]
    picked_ref[...] = jnp.broadcast_to(column(mask_ref), picked_ref.shape)
    for place, vector_ref in enumerate((bo_ref, gain_ref, shift_ref)):
        norm_ref[place : place + 1, :] = vector_ref[...].astype(F32)[None]
    own_bias = bias_row(slab, own_span(len_ref, slab))
    bias_ref[:, :slab] = jnp.broadcast_to(own_bias, (bias_ref.shape[0], slab))
    kept = slab - SHORTEST
    bias_ref[:, slab:] = jnp.broadcast_to(
        bias_row(kept, peer_span(len_ref, kept)), (bias_ref.shape[0], kept)
    )
    rows = x_ref[...]
    stacked = stack_queries(rows, wq_ref, bq_ref)
    q_ref[...] = stacked
    new_k = project(rows, wk_ref, bk_ref)
    new_v = project(rows, wv_ref, bv_ref)
    kt_ref[...] = k_ref[...].T
    s_own = mm(stacked, kt_ref[...]) + own_bias
    s_new = mm_t(stacked, new_k)
    top = jnp.maximum(jnp.max(s_own, -1, keepdims=True), jnp.max(s_new, -1, keepdims=True))
    e_own = jnp.exp2(s_own - top)
    e_new = jnp.exp2(s_new - top)
    total = jnp.sum(e_own, -1, keepdims=True) + jnp.sum(e_new, -1, keepdims=True)
    acc_ref[...] = mm(e_own.astype(BF16), v_ref[...]) + mm(e_new.astype(BF16), new_v)
    max_ref[...] = jnp.broadcast_to(top, max_ref.shape)
    sum_ref[...] = jnp.broadcast_to(total, sum_ref.shape)


def send_kernel(slab_hbm, out_ref, sem):
    kept = out_ref.shape[0]
    first = pl.multiple_of(
        jnp.where(lax.axis_index("group") % 2 == 0, slab_hbm.shape[0] - kept, 0), SHORTEST
    )
    load = pltpu.make_async_copy(slab_hbm.at[pl.ds(first, kept)], out_ref, sem)
    load.start()
    load.wait()


def peer_score_kernel(
    bias_ref, q_ref, k_ref, acc_ref, max_ref, sum_ref, e_ref, out_ref, total_ref, kt_ref
):
    kept = k_ref.shape[0]
    kt_ref[...] = k_ref[...].T
    scores = mm(q_ref[...], kt_ref[...]) + bias_ref[0:1, bias_ref.shape[1] - kept :]
    before = max_ref[:, :1]
    top = jnp.maximum(before, jnp.max(scores, -1, keepdims=True))
    expo = jnp.exp2(scores - top)
    shrink = jnp.exp2(before - top)
    total = sum_ref[:, :1] * shrink + jnp.sum(expo, -1, keepdims=True)
    e_ref[...] = expo.astype(BF16)
    out_ref[...] = acc_ref[...] * shrink
    total_ref[...] = jnp.broadcast_to(total, total_ref.shape)


def peer_value_kernel(e_ref, v_ref, acc_ref, total_ref, att_ref):
    summed = acc_ref[...] + mm(e_ref[...], v_ref[...])
    att_ref[...] = unstack_heads(summed / total_ref[:, :1], att_ref.shape[0]).astype(BF16)


def out_project(att_ref, wo_refs, rows, norm_ref):
    summed = norm_ref[0:1, :] + rows.astype(F32)
    me = lax.axis_index("tensor")
    for apart, wo_ref in enumerate(wo_refs):
        summed += mm(att_ref[me ^ apart], wo_ref[...])
    return layer_norm(summed, norm_ref)


def second_kernel(
    bias_ref, att_ref, wo0, wo1, wo2, wo3, norm_ref, x_ref, picked_ref,
    wq_ref, wk_ref, wv_ref, bq_ref, bk_ref, bv_ref, kt_ref, v_ref, pkt_ref, pv_ref,
    second_ref, att_out_ref, s_ref, e_ref,
):
    block = x_ref[...]
    first = out_project(att_ref, (wo0, wo1, wo2, wo3), block, norm_ref)
    rows = jnp.where(picked_ref[:, :1] == 1, first, block)
    second_ref[...] = rows
    stacked = stack_queries(rows, wq_ref, bq_ref)
    own, cached = kt_ref.shape[1], kt_ref.shape[1] + pkt_ref.shape[1]
    s_ref[:, :own] = mm(stacked, kt_ref[...])
    s_ref[:, own:cached] = mm(stacked, pkt_ref[...])
    new_k = project(rows, wk_ref, bk_ref)
    new_v = project(rows, wv_ref, bv_ref)
    s_ref[:, cached:] = mm_t(stacked, new_k)
    bias = bias_ref[0:1, :]
    count = rows.shape[0]
    head_of = lax.broadcasted_iota(jnp.int32, att_out_ref.shape, 1) // HD
    merged = jnp.zeros(att_out_ref.shape, F32)
    for head in range(stacked.shape[0] // count):
        sums = []
        for low in range(head * count, (head + 1) * count, STEP):
            at = slice(low, low + STEP)
            s_old = s_ref[at, :cached] + bias
            s_new = s_ref[at, cached:]
            top = jnp.maximum(jnp.max(s_old, -1, keepdims=True), jnp.max(s_new, -1, keepdims=True))
            e_old = jnp.exp2(s_old - top)
            e_new = jnp.exp2(s_new - top)
            sums.append(jnp.sum(e_old, -1, keepdims=True) + jnp.sum(e_new, -1, keepdims=True))
            e_ref[at, :cached] = e_old.astype(BF16)
            e_ref[at, cached:] = e_new.astype(BF16)
        at = slice(head * count, (head + 1) * count)
        summed = (
            mm(e_ref[at, :own], v_ref[...])
            + mm(e_ref[at, own:cached], pv_ref[...])
            + mm(e_ref[at, cached:], new_v)
        ) / jnp.concatenate(sums, 0)
        merged = jnp.where(head_of == head, summed, merged)
    att_out_ref[...] = merged.astype(BF16)


def last_kernel(att_ref, wo0, wo1, wo2, wo3, norm_ref, x_ref, out_ref):
    out_ref[...] = out_project(
        att_ref, (wo0, wo1, wo2, wo3), x_ref[...], norm_ref
    )


def call(kernel, name, outs, *args, in_hbm=(), scratch=(), flops=1 << 10, limit=24):
    specs = [
        pl.BlockSpec(memory_space=pltpu.SMEM if arg.dtype == jnp.int32 and arg.ndim == 1 else pltpu.VMEM)
        for arg in args
    ] + [pl.BlockSpec(memory_space=pltpu.HBM)] * len(in_hbm)
    return pl.pallas_call(
        kernel,
        name=name,
        out_shape=outs,
        in_specs=specs,
        out_specs=jax.tree.map(lambda _: pl.BlockSpec(memory_space=pltpu.VMEM), outs),
        scratch_shapes=scratch,
        compiler_params=pltpu.CompilerParams(vmem_limit_bytes=limit * MIB),
        cost_estimate=pl.CostEstimate(flops=flops, bytes_accessed=1 << 10, transcendentals=0),
    )(*args, *in_hbm)


def after(array, other):
    return lax.optimization_barrier((array, other))[0]


def moved(array, axis, apart):
    return lax.ppermute(array, axis, [(i, i ^ apart) for i in range(lax.axis_size(axis))])


def body(
    block, mask, cache_len, cache_k, cache_v, w_q, b_q, w_k, b_k, w_v, b_v, w_o, b_o, ln_gain, ln_shift
):
    rows = block[0]
    own_k, own_v = cache_k[0], cache_v[0]
    slab, width = own_k.shape
    count = rows.shape[0]
    stack = count * (width // HD)

    shape = jax.ShapeDtypeStruct
    dma = pltpu.SemaphoreType.DMA

    def sendable(array, name):
        return call(
            send_kernel, name, shape((slab - SHORTEST, width), BF16), in_hbm=(array,), scratch=[dma]
        )

    send_k = sendable(own_k, "send_k")
    send_v = sendable(after(own_v, send_k), "send_v")
    peer_k = moved(send_k, "group", 1)
    peer_v = moved(send_v, "group", 1)
    wo2 = moved(w_o, "tensor", 2)
    stats = shape((stack, 128), F32)
    q_stack, acc, top, total, picked, norm, bias, own_kt = call(
        own_kernel, "own",
        (shape((stack, width), BF16), shape((stack, width), F32), stats, stats, shape((count, 128), jnp.int32), shape((8, rows.shape[1]), F32),
         shape((8, 2 * slab - SHORTEST), F32), shape((width, slab), BF16)),
        cache_len, mask, rows, w_q, w_k, w_v, b_q, b_k, b_v, own_k, own_v,
        b_o, ln_gain, ln_shift,
    )
    wo1 = moved(after(w_o, acc), "tensor", 1)
    expo, acc, total, peer_kt = call(
        peer_score_kernel, "peer_score",
        (shape((stack, slab - SHORTEST), BF16), shape((stack, width), F32), stats,
         shape((width, slab - SHORTEST), BF16)),
        bias, q_stack, peer_k, acc, top, total, flops=1 << 33,
    )
    wo3 = moved(after(wo2, expo), "tensor", 1)
    wo = (w_o, wo1, wo2, wo3)
    att = call(peer_value_kernel, "peer_value", shape((count, width), BF16), expo, peer_v, acc, total)
    att = lax.all_gather(att, "tensor")
    second, att = call(
        second_kernel, "second",
        (shape(rows.shape, BF16), shape((count, width), BF16)),
        bias, att, *wo, norm, rows, picked,
        w_q, w_k, w_v, b_q, b_k, b_v, own_kt, own_v, peer_kt, peer_v,
        scratch=[pltpu.VMEM((stack, 2 * slab), F32), pltpu.VMEM((stack, 2 * slab), BF16)],
    )
    att = lax.all_gather(att, "tensor")
    out = call(
        last_kernel, "last", shape(rows.shape, BF16),
        att, *wo, norm, second,
    )
    return out[None]


def solution(mesh):
    return jax.shard_map(
        body,
        mesh=mesh,
        in_specs=(
            P("group", None, None),
            P("group", None),
            P(),
            P("group", None, "tensor"),
            P("group", None, "tensor"),
            P(None, "tensor"),
            P("tensor"),
            P(None, "tensor"),
            P("tensor"),
            P(None, "tensor"),
            P("tensor"),
            P("tensor", None),
            P(),
            P(),
            P(),
        ),
        out_specs=P("group", None, None),
        check_vma=False,
    )
```

time: 56 us -> 45.3 us (0.81)
  local copies, waits for them, and re-layouts: 9.59 us -> 3.26 us
  between operations: 2.89 us -> 0.3 us
  Pallas kernels: 11.8 us -> 10.1 us
  starting transfers between devices: 18.5 us -> 19.5 us
  blocking collectives: 12.6 us -> 11.7 us
    unnamed x42 -> x34, local copies, waits for them, and re-layouts: 8.83 us -> 3.26 us
    pallas_call x5 -> x7, Pallas kernels: 11.8 us -> 10.1 us  [call(): pl.pallas_call(kernel, name=name, out_shape=outs, in_specs=specs, out_spe...]
    ppermute x5, starting transfers between devices: 18.5 us -> 19.5 us  [moved(): lax.ppermute(array, axis, [(i, i ^ apart) for i in range(lax.axis_size(ax...]
    all_gather x2, blocking collectives: 12.6 us -> 11.7 us  [body(): att = lax.all_gather(att, 'tensor')]
    dynamic_slice x1 -> x0, local copies, waits for them, and re-layouts: 0.58 us -> none  [body(): length = cache_len[group]]
  transfers between devices with their start and end apart: 5 -> 5, of which waited for: 0 -> 0; matrix products, arithmetic and copies ran while one was open for 0% -> 0% of each run, Pallas kernels for 10% -> 11%
where the time goes in v2:
time: 45.3 us; the launch traced here: 44.9 us
  starting transfers between devices  19.5 us (43%)
  blocking collectives  11.7 us (26%)
  Pallas kernels  10.1 us (22%)
  local copies, waits for them, and re-layouts  3.26 us (7%)
    ppermute x5, starting transfers between devices, moved(): lax.ppermute(array, axis, [(i, i ^ apart) for i in range(lax.axis_size(ax...  19.5 us
    all_gather x2, blocking collectives, body(): att = lax.all_gather(att, 'tensor')  11.7 us
    pallas_call x7, Pallas kernels, call(): pl.pallas_call(kernel, name=name, out_shape=outs, in_specs=specs, out_spe...  10.1 us
    unnamed x34, local copies, waits for them, and re-layouts  3.26 us
  transfers between devices with their start and end apart: 5, of which 0 were waited for; matrix products, arithmetic and copies ran while one was open for 0% of the time, Pallas kernels for 11%

profile of v2, /device:TPU:1, one launch (start us, length us, event | category | flops | bytes accessed | tf_op | source)
XLA Modules:
  0.0 44.9 jit_solution(3484564794329747864)
XLA Ops:
  0.0 0.0 copy-start
  0.0 0.0 copy-start.5
  0.0 1.1 %copy-done.5 = bf16[1,1024,256]{2,1,0:T(8,128)(2,1)S(1)} copy-done((bf16[1,1024,256]{2,1,0:T(8,128)(2,1)S(1)}, bf16[1,1024,256]{2,1,0:T(8,128)(2,1)}, u32[]{:S(2)}) %copy-start.5) | copy-done | bytes 524312
  1.1 0.0 copy-start.2
  1.1 0.3 send_k.1
  1.4 0.0 copy-start.1
  1.4 4.1 %collective-permute-start = (bf16[896,256]{1,0:T(8,128)(2,1)S(1)}, bf16[896,256]{1,0:T(8,128)(2,1)S(1)}, u32[]{:S(2)}, u32[]{:S(2)}) collective-permute-start(bf16[896,256]{1,0:T(8,128)(2,1)S(1)} %send_k.1), channel_id=1, source_target_pairs={{0,4},{4,0},{8,12},{12,8},{16,20},{20,16},{24,28},{28,24},{32,36},... | collective-permute-start | bytes 1376264 | tf_op jit(solution)/shard_map/ppermute | solution.py:228
  5.5 0.0 copy-done
  5.5 0.0 copy-start.8
  5.5 0.0 copy-start.9
  5.5 0.0 copy-start.10
  5.5 0.0 copy-start.11
  5.5 0.0 copy-start.15
  5.6 0.0 copy-start.16
  5.6 0.3 send_v.1
  5.9 0.0 copy-start.12
  5.9 0.0 copy-start.13
  5.9 0.0 copy-start.14
  5.9 2.1 %collective-permute-start.1 = (bf16[896,256]{1,0:T(8,128)(2,1)S(1)}, bf16[896,256]{1,0:T(8,128)(2,1)S(1)}, u32[]{:S(2)}, u32[]{:S(2)}) collective-permute-start(bf16[896,256]{1,0:T(8,128)(2,1)S(1)} %send_v.1), channel_id=1, source_target_pairs={{0,4},{4,0},{8,12},{12,8},{16,20},{20,16},{24,28},{28,24},{32,36},... | collective-permute-start | bytes 1376264 | tf_op jit(solution)/shard_map/ppermute | solution.py:228
  8.0 3.4 %collective-permute-start.3 = (bf16[256,1024]{1,0:T(8,128)(2,1)}, bf16[256,1024]{1,0:T(8,128)(2,1)S(1)}, u32[]{:S(2)}, u32[]{:S(2)}) collective-permute-start(bf16[256,1024]{1,0:T(8,128)(2,1)} %wo0.3), channel_id=1, source_target_pairs={{0,2},{1,3},{2,0},{3,1},{4,6},{5,7},{6,4},{7,5},{8,10},{9,11},{10,... | collective-permute-start | bytes 1572872 | tf_op jit(solution)/shard_map/ppermute | solution.py:228
  11.4 0.0 copy-done.2
  11.4 0.0 copy-done.1
  11.5 0.0 copy-done.8
  11.5 0.0 copy-done.9
  11.5 0.0 copy-done.10
  11.5 0.0 copy-done.11
  11.5 0.0 copy-done.15
  11.5 0.0 copy-done.16
  11.5 0.0 copy-done.12
  11.5 0.0 copy-done.13
  11.5 0.0 copy-done.14
  11.5 0.0 copy-start.3
  11.6 1.0 %copy-done.3 = bf16[1024,256]{1,0:T(8,128)(2,1)S(1)} copy-done((bf16[1024,256]{1,0:T(8,128)(2,1)S(1)}, bf16[1024,256]{1,0:T(8,128)(2,1)}, u32[]{:S(2)}) %copy-start.3) | copy-done | bytes 524312
  12.6 0.0 copy-start.6
  12.6 1.0 %copy-done.6 = bf16[1,1024,256]{2,1,0:T(8,128)(2,1)S(1)} copy-done((bf16[1,1024,256]{2,1,0:T(8,128)(2,1)S(1)}, bf16[1,1024,256]{2,1,0:T(8,128)(2,1)}, u32[]{:S(2)}) %copy-start.6) | copy-done | bytes 524312
  13.6 0.0 copy-start.7
  13.6 2.5 %own.1 = (bf16[512,256]{1,0:T(8,128)(2,1)S(1)}, f32[512,256]{1,0:T(8,128)S(1)}, f32[512,128]{1,0:T(8,128)S(1)}, f32[512,128]{1,0:T(8,128)S(1)}, s32[128,128]{1,0...) custom-call(s32[128]{0:T(128)S(1)} %copy-done.15, ...), custom_call_target="tpu_custom_call" | custom-call | flops 1024 | bytes 1024 | tf_op jit(solution)/shard_map/own/pallas_call | solution.py:211
  16.1 0.0 copy-done.7
  16.1 7.2 %collective-permute-start.2 = (bf16[256,1024]{1,0:T(8,128)(2,1)S(1)}, bf16[256,1024]{1,0:T(8,128)(2,1)S(1)}, u32[]{:S(2)}, u32[]{:S(2)}) collective-permute-start(bf16[256,1024]{1,0:T(8,128)(2,1)S(1)} %copy-done.7), channel_id=1, source_target_pairs={{0,1},{1,0},{2,3},{3,2},{4,5},{5,4},{6,7},{7,6},{8,9},{9,8},{10,11... | collective-permute-start | bytes 1572872 | tf_op jit(solution)/shard_map/ppermute | solution.py:228
  23.4 0.0 collective-permute-done.k_ref
  23.4 1.9 %peer_score.1 = (bf16[512,896]{1,0:T(8,128)(2,1)S(1)}, f32[512,256]{1,0:T(8,128)S(1)}, f32[512,128]{1,0:T(8,128)S(1)}, bf16[256,896]{1,0:T(8,128)(2,1)S(1)}) custom-call(f32[8,1920]{1,0:T(8,128)S(1)} %get-tuple-element.22.bias_ref, bf16[512,256]{1,0:T(8,128)(2,1)S(1)} %get-tuple-element.23.q_ref, bf16[896,256]{1,0:T(8,128)(2,1)S(1)} %collective-permute-done.k_ref, ...), custom_call_target="tpu_custom_call" | custom-call | flops 8589934592 | bytes 1024 | tf_op jit(solution)/shard_map/peer_score/pallas_call | solution.py:211
  25.3 0.0 collective-permute-done.3.wo2
  25.3 2.7 %collective-permute-start.4 = (bf16[256,1024]{1,0:T(8,128)(2,1)S(1)}, bf16[256,1024]{1,0:T(8,128)(2,1)S(1)}, u32[]{:S(2)}, u32[]{:S(2)}) collective-permute-start(bf16[256,1024]{1,0:T(8,128)(2,1)S(1)} %collective-permute-done.3.wo2), channel_id=1, source_target_pairs={{0,1},{1,0},{2,3},{3,2},{4,5},{5,4},{6,7},{7,6},{8,9},{9,8},{10,11... | collective-permute-start | bytes 1572872 | tf_op jit(solution)/shard_map/ppermute | solution.py:228
  28.0 0.0 collective-permute-done.1.v_ref.pv_ref
  28.0 0.0 copy-start.4
  28.0 0.4 peer_value.1
  28.5 5.9 %all-gather = bf16[512,256]{1,0:T(8,128)(2,1)S(1)} all-gather(bf16[128,256]{1,0:T(8,128)(2,1)S(1)} %peer_value.1), channel_id=2, replica_groups=mesh['group'=128,'tensor'=4] {'tensor'}, dimensions={0}, use_global_device_ids=true | all-gather | bytes 327680 | tf_op jit(solution)/shard_map/all_gather | solution.py:271
  34.4 0.0 collective-permute-done.2.wo1
  34.4 0.0 collective-permute-done.4.wo3
  34.4 0.0 copy-done.4
  34.4 3.3 %second.1 = (bf16[128,1024]{1,0:T(8,128)(2,1)S(1)}, bf16[128,256]{1,0:T(8,128)(2,1)S(1)}) custom-call(f32[8,1920]{1,0:T(8,128)S(1)} %get-tuple-element.22.bias_ref, bf16[4,128,256]{2,1,0:T(8,128)(2,1)S(1)} %bitcast.13, bf16[256,1024]{1,0:T(8,128)(2,1)S(1)} %copy-done.7, bf16[256,1024]{1,0:T(8,128)(2,1)S(1)} %collective-permute-done.2.wo1, ...), custom_call_target="tpu_custom_call" | custom-call | flops 1024 | bytes 1024 | tf_op jit(solution)/shard_map/second/pallas_call | solution.py:211
  37.6 5.9 %all-gather.1 = bf16[512,256]{1,0:T(8,128)(2,1)S(1)} all-gather(bf16[128,256]{1,0:T(8,128)(2,1)S(1)} %get-tuple-element.37), channel_id=3, replica_groups=mesh['group'=128,'tensor'=4] {'tensor'}, dimensions={0}, use_global_device_ids=true | all-gather | bytes 327680 | tf_op jit(solution)/shard_map/all_gather | solution.py:279
  43.5 1.4 %last.1 = bf16[128,1024]{1,0:T(8,128)(2,1)} custom-call(bf16[4,128,256]{2,1,0:T(8,128)(2,1)S(1)} %bitcast.14, bf16[256,1024]{1,0:T(8,128)(2,1)S(1)} %copy-done.7, bf16[256,1024]{1,0:T(8,128)(2,1)S(1)} %collective-permute-done.2.wo1, bf16[256,1024]{1,0:T(8,128)(2,1)S(1)} %collective-permute-done.3.wo2, bf16[256,1024]{1,0:T(8,128)(2,1)S(1)} %collective-permute-done.4.wo3, ...), custom_call_target="tpu_custom_call" | custom-call | flops 1024 | bytes 1024 | tf_op jit(solution)/shard_map/last/pallas_call | solution.py:211
Async XLA Ops:
  0.0 5.5 %copy-start = (bf16[1,1024,256]{2,1,0:T(8,128)(2,1)S(1)}, bf16[1,1024,256]{2,1,0:T(8,128)(2,1)}, u32[]{:S(2)}) copy-start(bf16[1,1024,256]{2,1,0:T(8,128)(2,1)} %param.19) | copy-start | bytes 1572868
  0.0 1.1 %copy-start.5 = (bf16[1,1024,256]{2,1,0:T(8,128)(2,1)S(1)}, bf16[1,1024,256]{2,1,0:T(8,128)(2,1)}, u32[]{:S(2)}) copy-start(bf16[1,1024,256]{2,1,0:T(8,128)(2,1)} %param.18) | copy-start | bytes 1572868
  1.1 10.3 %copy-start.2 = (bf16[1024,256]{1,0:T(8,128)(2,1)S(1)}, bf16[1024,256]{1,0:T(8,128)(2,1)}, u32[]{:S(2)}) copy-start(bf16[1024,256]{1,0:T(8,128)(2,1)} %wk_ref.3) | copy-start | bytes 1572868
  1.4 10.1 %copy-start.1 = (bf16[1024,256]{1,0:T(8,128)(2,1)S(1)}, bf16[1024,256]{1,0:T(8,128)(2,1)}, u32[]{:S(2)}) copy-start(bf16[1024,256]{1,0:T(8,128)(2,1)} %wq_ref.3) | copy-start | bytes 1572868
  1.4 22.0 %collective-permute-start = (bf16[896,256]{1,0:T(8,128)(2,1)S(1)}, bf16[896,256]{1,0:T(8,128)(2,1)S(1)}, u32[]{:S(2)}, u32[]{:S(2)}) collective-permute-start(bf16[896,256]{1,0:T(8,128)(2,1)S(1)} %send_k.1), channel_id=1, source_target_pairs={{0,4},{4,0},{8,12},{12,8},{16,20},{20,16},{24,28},{28,24},{32,36},... | collective-permute-start | bytes 1376264 | tf_op jit(solution)/shard_map/ppermute | solution.py:228
  5.5 6.0 %copy-start.8 = (bf16[1,128,1024]{2,1,0:T(8,128)(2,1)S(1)}, bf16[1,128,1024]{2,1,0:T(8,128)(2,1)}, u32[]{:S(2)}) copy-start(bf16[1,128,1024]{2,1,0:T(8,128)(2,1)} %param.15) | copy-start | bytes 786436
  5.5 6.0 %copy-start.9 = (bf16[1024]{0:T(1024)(128)(2,1)S(1)}, bf16[1024]{0:T(1024)(128)(2,1)}, u32[]{:S(2)}) copy-start(bf16[1024]{0:T(1024)(128)(2,1)} %bo_ref.1) | copy-start | bytes 6148
  5.5 6.0 %copy-start.10 = (bf16[1024]{0:T(1024)(128)(2,1)S(1)}, bf16[1024]{0:T(1024)(128)(2,1)}, u32[]{:S(2)}) copy-start(bf16[1024]{0:T(1024)(128)(2,1)} %gain_ref.1) | copy-start | bytes 6148
  5.5 5.9 %copy-start.11 = (bf16[1024]{0:T(1024)(128)(2,1)S(1)}, bf16[1024]{0:T(1024)(128)(2,1)}, u32[]{:S(2)}) copy-start(bf16[1024]{0:T(1024)(128)(2,1)} %shift_ref.1) | copy-start | bytes 6148
  5.5 5.9 %copy-start.15 = (s32[128]{0:T(128)S(1)}, s32[128]{0:T(128)}, u32[]{:S(2)}) copy-start(s32[128]{0:T(128)} %len_ref.1) | copy-start | bytes 1540
  5.6 5.9 %copy-start.16 = (s32[1,128]{1,0:T(1,128)S(1)}, s32[1,128]{1,0:T(1,128)}, u32[]{:S(2)}) copy-start(s32[1,128]{1,0:T(1,128)} %mask_ref.1) | copy-start | bytes 1540
  5.9 5.6 %copy-start.12 = (bf16[256]{0:T(256)(128)(2,1)S(1)}, bf16[256]{0:T(256)(128)(2,1)}, u32[]{:S(2)}) copy-start(bf16[256]{0:T(256)(128)(2,1)} %bq_ref.3) | copy-start | bytes 1540
  5.9 5.6 %copy-start.13 = (bf16[256]{0:T(256)(128)(2,1)S(1)}, bf16[256]{0:T(256)(128)(2,1)}, u32[]{:S(2)}) copy-start(bf16[256]{0:T(256)(128)(2,1)} %bk_ref.3) | copy-start | bytes 1540
  5.9 5.6 %copy-start.14 = (bf16[256]{0:T(256)(128)(2,1)S(1)}, bf16[256]{0:T(256)(128)(2,1)}, u32[]{:S(2)}) copy-start(bf16[256]{0:T(256)(128)(2,1)} %bv_ref.3) | copy-start | bytes 1540
  5.9 22.1 %collective-permute-start.1 = (bf16[896,256]{1,0:T(8,128)(2,1)S(1)}, bf16[896,256]{1,0:T(8,128)(2,1)S(1)}, u32[]{:S(2)}, u32[]{:S(2)}) collective-permute-start(bf16[896,256]{1,0:T(8,128)(2,1)S(1)} %send_v.1), channel_id=1, source_target_pairs={{0,4},{4,0},{8,12},{12,8},{16,20},{20,16},{24,28},{28,24},{32,36},... | collective-permute-start | bytes 1376264 | tf_op jit(solution)/shard_map/ppermute | solution.py:228
  8.0 17.3 %collective-permute-start.3 = (bf16[256,1024]{1,0:T(8,128)(2,1)}, bf16[256,1024]{1,0:T(8,128)(2,1)S(1)}, u32[]{:S(2)}, u32[]{:S(2)}) collective-permute-start(bf16[256,1024]{1,0:T(8,128)(2,1)} %wo0.3), channel_id=1, source_target_pairs={{0,2},{1,3},{2,0},{3,1},{4,6},{5,7},{6,4},{7,5},{8,10},{9,11},{10,... | collective-permute-start | bytes 1572872 | tf_op jit(solution)/shard_map/ppermute | solution.py:228
  11.5 1.0 %copy-start.3 = (bf16[1024,256]{1,0:T(8,128)(2,1)S(1)}, bf16[1024,256]{1,0:T(8,128)(2,1)}, u32[]{:S(2)}) copy-start(bf16[1024,256]{1,0:T(8,128)(2,1)} %wv_ref.3) | copy-start | bytes 1572868
  12.6 1.0 %copy-start.6 = (bf16[1,1024,256]{2,1,0:T(8,128)(2,1)S(1)}, bf16[1,1024,256]{2,1,0:T(8,128)(2,1)}, u32[]{:S(2)}) copy-start(bf16[1,1024,256]{2,1,0:T(8,128)(2,1)} %param.18) | copy-start | bytes 1572868
  13.6 2.5 %copy-start.7 = (bf16[256,1024]{1,0:T(8,128)(2,1)S(1)}, bf16[256,1024]{1,0:T(8,128)(2,1)}, u32[]{:S(2)}) copy-start(bf16[256,1024]{1,0:T(8,128)(2,1)} %wo0.3) | copy-start | bytes 1572868
  16.1 18.2 %collective-permute-start.2 = (bf16[256,1024]{1,0:T(8,128)(2,1)S(1)}, bf16[256,1024]{1,0:T(8,128)(2,1)S(1)}, u32[]{:S(2)}, u32[]{:S(2)}) collective-permute-start(bf16[256,1024]{1,0:T(8,128)(2,1)S(1)} %copy-done.7), channel_id=1, source_target_pairs={{0,1},{1,0},{2,3},{3,2},{4,5},{5,4},{6,7},{7,6},{8,9},{9,8},{10,11... | collective-permute-start | bytes 1572872 | tf_op jit(solution)/shard_map/ppermute | solution.py:228
  25.3 9.1 %collective-permute-start.4 = (bf16[256,1024]{1,0:T(8,128)(2,1)S(1)}, bf16[256,1024]{1,0:T(8,128)(2,1)S(1)}, u32[]{:S(2)}, u32[]{:S(2)}) collective-permute-start(bf16[256,1024]{1,0:T(8,128)(2,1)S(1)} %collective-permute-done.3.wo2), channel_id=1, source_target_pairs={{0,1},{1,0},{2,3},{3,2},{4,5},{5,4},{6,7},{7,6},{8,9},{9,8},{10,11... | collective-permute-start | bytes 1572872 | tf_op jit(solution)/shard_map/ppermute | solution.py:228
  28.0 6.3 %copy-start.4 = (bf16[1024,256]{1,0:T(8,128)(2,1)S(1)}, bf16[1024,256]{1,0:T(8,128)(2,1)}, u32[]{:S(2)}) copy-start(bf16[1024,256]{1,0:T(8,128)(2,1)} %wv_ref.3) | copy-start | bytes 1572868

commit v3 on v2

v3 whole, which is shorter than its diff:
```python
import jax
import jax.numpy as jnp
from jax import lax
from jax.experimental import pallas as pl
from jax.experimental.pallas import tpu as pltpu
from jax.sharding import PartitionSpec as P

HD = 64
SHORTEST = 128
NEG = -1e30
EPS = 1e-05
F32 = jnp.float32
BF16 = jnp.bfloat16
MIB = 1 << 20
LOG2E = 1.4426950408889634
STEP = 16


def mm(left, right):
    return jnp.dot(left, right, preferred_element_type=F32)


def mm_t(left, right):
    return lax.dot_general(left, right, (((1,), (1,)), ((), ())), preferred_element_type=F32)


def project(rows, w_ref, b_ref):
    return (mm(rows, w_ref[...]) + b_ref[...].astype(F32)[None]).astype(BF16)


def stack_queries(rows, w_ref, b_ref):
    scaled = (
        (mm(rows, w_ref[...]) + b_ref[...].astype(F32)[None]) * F32(LOG2E * HD**-0.5)
    ).astype(BF16)
    head_of = lax.broadcasted_iota(jnp.int32, scaled.shape, 1) // HD
    heads = scaled.shape[1] // HD
    return jnp.concatenate(
        [jnp.where(head_of == head, scaled, jnp.zeros_like(scaled)) for head in range(heads)], 0
    )


def unstack_heads(stacked, rows):
    heads = stacked.shape[0] // rows
    head_of = lax.broadcasted_iota(jnp.int32, (rows, stacked.shape[1]), 1) // HD
    merged = stacked[:rows]
    for head in range(1, heads):
        merged = jnp.where(head_of == head, stacked[head * rows : (head + 1) * rows], merged)
    return merged


def read_length(len_ref):
    group = lax.axis_index("group")
    place = lax.broadcasted_iota(jnp.int32, len_ref.shape, 1)
    return jnp.sum(jnp.where(place == group, len_ref[...], 0), -1, keepdims=True)


def own_span(length, slab):
    even = lax.axis_index("group") % 2 == 0
    return jnp.where(even, 0, slab - length), jnp.where(even, length, slab)


def peer_span(length, kept):
    beyond = length - (kept + SHORTEST)
    even = lax.axis_index("group") % 2 == 0
    return jnp.where(even, 0, kept - beyond), jnp.where(even, beyond, kept)


def bias_row(count, span):
    low, high = span
    place = lax.broadcasted_iota(jnp.int32, (1, count), 1)
    return jnp.where((place >= low) & (place < high), F32(0), F32(NEG))


def column(row_ref):
    count = row_ref.shape[1]
    square = jnp.broadcast_to(row_ref[...], (count, count))
    across = lax.broadcasted_iota(jnp.int32, square.shape, 1)
    down = lax.broadcasted_iota(jnp.int32, square.shape, 0)
    return jnp.sum(jnp.where(across == down, square, 0), -1, keepdims=True)


def layer_norm(summed, norm_ref):
    centre = summed - jnp.mean(summed, -1, keepdims=True)
    spread = jnp.mean(centre * centre, -1, keepdims=True)
    return (centre * lax.rsqrt(spread + EPS) * norm_ref[1:2, :] + norm_ref[2:3, :]).astype(BF16)


def chunks(low, high, step):
    return [slice(start, start + step) for start in range(low, high, step)]


def own_kernel(
    len_ref, mask_ref, x_ref, wq_ref, wk_ref, wv_ref, bq_ref, bk_ref, bv_ref, k_ref, v_ref,
    bo_ref, gain_ref, shift_ref,
    q_ref, acc_ref, stat_ref, picked_ref, norm_ref, bias_ref, kt_ref, s_ref, e_ref,
):
    slab, count = k_ref.shape[0], x_ref.shape[0]
    rows = x_ref[...]
    stacked = stack_queries(rows, wq_ref, bq_ref)
    q_ref[...] = stacked
    kt_ref[...] = k_ref[...].T
    s_ref[:, :slab] = mm(stacked, kt_ref[...])
    new_k = project(rows, wk_ref, bk_ref)
    new_v = project(rows, wv_ref, bv_ref)
    s_ref[:, slab:] = mm_t(stacked, new_k)
    length = read_length(len_ref)
    own_bias = bias_row(slab, own_span(length, slab))
    bias_ref[:, :slab] = jnp.broadcast_to(own_bias, (bias_ref.shape[0], slab))
    kept = slab - SHORTEST
    bias_ref[:, slab:] = jnp.broadcast_to(
        bias_row(kept, peer_span(length, kept)), (bias_ref.shape[0], kept)
    )
    picked_ref[...] = jnp.broadcast_to(column(mask_ref), picked_ref.shape)
    for place, vector_ref in enumerate((bo_ref, gain_ref, shift_ref)):
        norm_ref[place : place + 1, :] = vector_ref[...].astype(F32)[None]
    bias = bias_ref[0:1, :slab]
    half = stat_ref.shape[1] // 2
    for block in chunks(0, stacked.shape[0], count):
        for at in chunks(block.start, block.stop, STEP):
            s_old = s_ref[at, :slab] + bias
            s_new = s_ref[at, slab:]
            top = jnp.maximum(jnp.max(s_old, -1, keepdims=True), jnp.max(s_new, -1, keepdims=True))
            e_old = jnp.exp2(s_old - top)
            e_new = jnp.exp2(s_new - top)
            total = jnp.sum(e_old, -1, keepdims=True) + jnp.sum(e_new, -1, keepdims=True)
            e_ref[at, :slab] = e_old.astype(BF16)
            e_ref[at, slab:] = e_new.astype(BF16)
            stat_ref[at, :half] = jnp.broadcast_to(top, (STEP, half))
            stat_ref[at, half:] = jnp.broadcast_to(total, (STEP, half))
        acc_ref[block, :] = mm(e_ref[block, :slab], v_ref[...]) + mm(e_ref[block, slab:], new_v)


def send_kernel(slab_hbm, out_ref, sem):
    kept = out_ref.shape[0]
    first = pl.multiple_of(
        jnp.where(lax.axis_index("group") % 2 == 0, slab_hbm.shape[0] - kept, 0), SHORTEST
    )
    load = pltpu.make_async_copy(slab_hbm.at[pl.ds(first, kept)], out_ref, sem)
    load.start()
    load.wait()


def peer_score_kernel(
    bias_ref, q_ref, k_ref, acc_ref, stat_ref, e_ref, out_ref, scale_ref, kt_ref, s_ref, peer_ref
):
    kept = k_ref.shape[0]
    half = stat_ref.shape[1] // 2
    kt_ref[...] = k_ref[...].T
    bias = bias_ref[0:1, bias_ref.shape[1] - kept :]
    s_ref[...] = mm(q_ref[...], kt_ref[...])
    for at in chunks(0, q_ref.shape[0], STEP):
        scores = s_ref[at, :] + bias
        top = jnp.max(scores, -1, keepdims=True)
        expo = jnp.exp2(scores - top)
        e_ref[at, :] = expo.astype(BF16)
        peer_ref[at, :half] = jnp.broadcast_to(top, (STEP, half))
        peer_ref[at, half:] = jnp.broadcast_to(jnp.sum(expo, -1, keepdims=True), (STEP, half))
    top = jnp.maximum(stat_ref[:, :half], peer_ref[:, :half])
    own_part = jnp.exp2(stat_ref[:, :half] - top)
    peer_part = jnp.exp2(peer_ref[:, :half] - top)
    total = stat_ref[:, half:] * own_part + peer_ref[:, half:] * peer_part
    own_part, peer_part = own_part / total, peer_part / total
    for low in range(0, out_ref.shape[1], half):
        out_ref[:, low : low + half] = acc_ref[:, low : low + half] * own_part
    scale_ref[...] = peer_part


def peer_value_kernel(e_ref, v_ref, acc_ref, scale_ref, att_ref):
    summed = acc_ref[...] + mm(e_ref[...], v_ref[...]) * scale_ref[:, :1]
    att_ref[...] = unstack_heads(summed, att_ref.shape[0]).astype(BF16)


def out_project(att_ref, wo_refs, sum_ref):
    me = lax.axis_index("tensor")
    summed = mm(att_ref[me], wo_refs[0][...])
    for apart, wo_ref in enumerate(wo_refs[1:], 1):
        summed += mm(att_ref[me ^ apart], wo_ref[...])
    sum_ref[...] = summed


def sublayer(sum_ref, x_ref, norm_ref, at):
    return layer_norm(sum_ref[at, :] + norm_ref[0:1, :] + x_ref[at, :].astype(F32), norm_ref)


def second_kernel(
    bias_ref, att_ref, wo0, wo1, wo2, wo3, norm_ref, x_ref, picked_ref,
    wq_ref, wk_ref, wv_ref, bq_ref, bk_ref, bv_ref, kt_ref, v_ref, pkt_ref, pv_ref,
    second_ref, att_out_ref, s_ref, e_ref, sum_ref,
):
    count = x_ref.shape[0]
    out_project(att_ref, (wo0, wo1, wo2, wo3), sum_ref)
    for at in chunks(0, count, STEP):
        first = sublayer(sum_ref, x_ref, norm_ref, at)
        second_ref[at, :] = jnp.where(picked_ref[at, :1] == 1, first, x_ref[at, :])
    rows = second_ref[...]
    stacked = stack_queries(rows, wq_ref, bq_ref)
    own, cached = kt_ref.shape[1], kt_ref.shape[1] + pkt_ref.shape[1]
    s_ref[:, :own] = mm(stacked, kt_ref[...])
    s_ref[:, own:cached] = mm(stacked, pkt_ref[...])
    new_k = project(rows, wk_ref, bk_ref)
    new_v = project(rows, wv_ref, bv_ref)
    s_ref[:, cached:] = mm_t(stacked, new_k)
    bias = bias_ref[0:1, :]
    head_of = lax.broadcasted_iota(jnp.int32, att_out_ref.shape, 1) // HD
    merged = jnp.zeros(att_out_ref.shape, F32)
    for head, block in enumerate(chunks(0, stacked.shape[0], count)):
        sums = []
        for at in chunks(block.start, block.stop, STEP):
            s_old = s_ref[at, :cached] + bias
            s_new = s_ref[at, cached:]
            top = jnp.maximum(jnp.max(s_old, -1, keepdims=True), jnp.max(s_new, -1, keepdims=True))
            e_old = jnp.exp2(s_old - top)
            e_new = jnp.exp2(s_new - top)
            sums.append(jnp.sum(e_old, -1, keepdims=True) + jnp.sum(e_new, -1, keepdims=True))
            e_ref[at, :cached] = e_old.astype(BF16)
            e_ref[at, cached:] = e_new.astype(BF16)
        summed = (
            mm(e_ref[block, :own], v_ref[...])
            + mm(e_ref[block, own:cached], pv_ref[...])
            + mm(e_ref[block, cached:], new_v)
        ) / jnp.concatenate(sums, 0)
        merged = jnp.where(head_of == head, summed, merged)
    att_out_ref[...] = merged.astype(BF16)


def last_kernel(att_ref, wo0, wo1, wo2, wo3, norm_ref, x_ref, out_hbm, sum_ref, out_ref, sems):
    count = x_ref.shape[0]
    pieces = sems.shape[0]
    out_project(att_ref, (wo0, wo1, wo2, wo3), sum_ref)
    stores = []
    for piece, part in enumerate(chunks(0, count, count // pieces)):
        for at in chunks(part.start, part.stop, STEP):
            out_ref[at, :] = sublayer(sum_ref, x_ref, norm_ref, at)
        stores.append(pltpu.make_async_copy(out_ref.at[part], out_hbm.at[part], sems.at[piece]))
        stores[-1].start()
    for store in stores:
        store.wait()


def call(kernel, name, outs, *args, in_hbm=(), scratch=(), flops=1 << 10, limit=24, out_space=pltpu.VMEM):
    specs = [pl.BlockSpec(memory_space=pltpu.VMEM)] * len(args) + [pl.BlockSpec(memory_space=pltpu.HBM)] * len(in_hbm)
    return pl.pallas_call(
        kernel,
        name=name,
        out_shape=outs,
        in_specs=specs,
        out_specs=jax.tree.map(lambda _: pl.BlockSpec(memory_space=out_space), outs),
        scratch_shapes=scratch,
        compiler_params=pltpu.CompilerParams(vmem_limit_bytes=limit * MIB),
        cost_estimate=pl.CostEstimate(flops=flops, bytes_accessed=1 << 10, transcendentals=0),
    )(*args, *in_hbm)


def after(array, other):
    return lax.optimization_barrier((array, other))[0]


def moved(array, axis, apart):
    return lax.ppermute(array, axis, [(i, i ^ apart) for i in range(lax.axis_size(axis))])


def body(
    block, mask, cache_len, cache_k, cache_v, w_q, b_q, w_k, b_k, w_v, b_v, w_o, b_o, ln_gain, ln_shift
):
    rows = block[0]
    own_k, own_v = cache_k[0], cache_v[0]
    slab, width = own_k.shape
    count = rows.shape[0]
    stack = count * (width // HD)

    shape = jax.ShapeDtypeStruct
    dma = pltpu.SemaphoreType.DMA

    def sendable(array, name):
        return call(
            send_kernel, name, shape((slab - SHORTEST, width), BF16), in_hbm=(array,), scratch=[dma]
        )

    send_k = sendable(own_k, "send_k")
    send_v = sendable(after(own_v, send_k), "send_v")
    peer_k = moved(send_k, "group", 1)
    peer_v = moved(send_v, "group", 1)
    wo2 = moved(w_o, "tensor", 2)
    q_stack, acc, stats, picked, norm, bias, own_kt = call(
        own_kernel, "own",
        (shape((stack, width), BF16), shape((stack, width), F32), shape((stack, 256), F32),
         shape((count, 128), jnp.int32), shape((8, rows.shape[1]), F32),
         shape((8, 2 * slab - SHORTEST), F32), shape((width, slab), BF16)),
        cache_len.reshape(1, -1), mask, rows, w_q, w_k, w_v, b_q, b_k, b_v, own_k, own_v,
        b_o, ln_gain, ln_shift,
        scratch=[pltpu.VMEM((stack, slab + count), F32), pltpu.VMEM((stack, slab + count), BF16)],
    )
    wo1 = moved(after(w_o, acc), "tensor", 1)
    expo, acc, total, peer_kt = call(
        peer_score_kernel, "peer_score",
        (shape((stack, slab - SHORTEST), BF16), shape((stack, width), F32), shape((stack, 128), F32),
         shape((width, slab - SHORTEST), BF16)),
        bias, q_stack, peer_k, acc, stats, flops=1 << 33,
        scratch=[pltpu.VMEM((stack, slab - SHORTEST), F32), pltpu.VMEM((stack, 256), F32)],
    )
    wo3 = moved(after(wo2, expo), "tensor", 1)
    wo = (w_o, wo1, wo2, wo3)
    att = call(peer_value_kernel, "peer_value", shape((count, width), BF16), expo, peer_v, acc, total)
    att = lax.all_gather(att, "tensor")
    second, att = call(
        second_kernel, "second",
        (shape(rows.shape, BF16), shape((count, width), BF16)),
        bias, att, *wo, norm, rows, picked,
        w_q, w_k, w_v, b_q, b_k, b_v, own_kt, own_v, peer_kt, peer_v,
        scratch=[pltpu.VMEM((stack, 2 * slab), F32), pltpu.VMEM((stack, 2 * slab), BF16),
                 pltpu.VMEM(rows.shape, F32)],
    )
    att = lax.all_gather(att, "tensor")
    out = call(
        last_kernel, "last", shape(rows.shape, BF16), att, *wo, norm, second, out_space=pl.ANY,
        scratch=[pltpu.VMEM(rows.shape, F32), pltpu.VMEM(rows.shape, BF16), dma((4,))],
    )
    return out[None]


def solution(mesh):
    return jax.shard_map(
        body,
        mesh=mesh,
        in_specs=(
            P("group", None, None),
            P("group", None),
            P(),
            P("group", None, "tensor"),
            P("group", None, "tensor"),
            P(None, "tensor"),
            P("tensor"),
            P(None, "tensor"),
            P("tensor"),
            P(None, "tensor"),
            P("tensor"),
            P("tensor", None),
            P(),
            P(),
            P(),
        ),
        out_specs=P("group", None, None),
        check_vma=False,
    )
```

time: 45.3 us -> 45.1 us (level)
  Pallas kernels: 10.1 us -> 8.29 us
  starting transfers between devices: 19.5 us -> 20.5 us
  local copies, waits for them, and re-layouts: 3.26 us -> 3.83 us
    pallas_call x7, Pallas kernels: 10.1 us -> 8.29 us  [call(): pl.pallas_call(kernel, name=name, out_shape=outs, in_specs=specs, out_spe...]
    ppermute x5, starting transfers between devices: 19.5 us -> 20.5 us  [moved(): lax.ppermute(array, axis, [(i, i ^ apart) for i in range(lax.axis_size(ax...]
    unnamed x34, local copies, waits for them, and re-layouts: 3.26 us -> 3.83 us
  transfers between devices with their start and end apart: 5 -> 5, of which waited for: 0 -> 0; matrix products, arithmetic and copies ran while one was open for 0% -> 0% of each run, Pallas kernels for 11% -> 8%
where the time goes in v3:
time: 45.1 us; the launch traced here: 44.7 us
  starting transfers between devices  20.5 us (45%)
  blocking collectives  11.7 us (26%)
  Pallas kernels  8.29 us (18%)
  local copies, waits for them, and re-layouts  3.83 us (8%)
    ppermute x5, starting transfers between devices, moved(): lax.ppermute(array, axis, [(i, i ^ apart) for i in range(lax.axis_size(ax...  20.5 us
    all_gather x2, blocking collectives, body(): att = lax.all_gather(att, 'tensor')  11.7 us
    pallas_call x7, Pallas kernels, call(): pl.pallas_call(kernel, name=name, out_shape=outs, in_specs=specs, out_spe...  8.29 us
    unnamed x34, local copies, waits for them, and re-layouts  3.83 us
  transfers between devices with their start and end apart: 5, of which 0 were waited for; matrix products, arithmetic and copies ran while one was open for 0% of the time, Pallas kernels for 8%

profile of v3, /device:TPU:1, one launch (start us, length us, event | category | flops | bytes accessed | tf_op | source)
XLA Modules:
  0.0 44.7 jit_solution(11754415346591220919)
XLA Ops:
  0.0 0.0 copy-start
  0.0 0.0 copy-start.5
  0.0 1.1 %copy-done.5 = bf16[1,1024,256]{2,1,0:T(8,128)(2,1)S(1)} copy-done((bf16[1,1024,256]{2,1,0:T(8,128)(2,1)S(1)}, bf16[1,1024,256]{2,1,0:T(8,128)(2,1)}, u32[]{:S(2)}) %copy-start.5) | copy-done | bytes 524312
  1.1 0.0 copy-start.2
  1.1 0.3 send_k.1
  1.4 0.0 copy-start.1
  1.4 4.1 %collective-permute-start = (bf16[896,256]{1,0:T(8,128)(2,1)S(1)}, bf16[896,256]{1,0:T(8,128)(2,1)S(1)}, u32[]{:S(2)}, u32[]{:S(2)}) collective-permute-start(bf16[896,256]{1,0:T(8,128)(2,1)S(1)} %send_k.1), channel_id=1, source_target_pairs={{0,4},{4,0},{8,12},{12,8},{16,20},{20,16},{24,28},{28,24},{32,36},... | collective-permute-start | bytes 1376264 | tf_op jit(solution)/shard_map/ppermute | solution.py:259
  5.5 0.0 copy-done
  5.5 0.0 copy-start.8
  5.5 0.0 copy-start.10
  5.5 0.0 copy-start.11
  5.5 0.0 copy-start.15
  5.5 0.0 copy-start.16
  5.6 0.3 send_v.1
  5.9 0.0 copy-start.9
  5.9 1.9 %collective-permute-start.1 = (bf16[896,256]{1,0:T(8,128)(2,1)S(1)}, bf16[896,256]{1,0:T(8,128)(2,1)S(1)}, u32[]{:S(2)}, u32[]{:S(2)}) collective-permute-start(bf16[896,256]{1,0:T(8,128)(2,1)S(1)} %send_v.1), channel_id=1, source_target_pairs={{0,4},{4,0},{8,12},{12,8},{16,20},{20,16},{24,28},{28,24},{32,36},... | collective-permute-start | bytes 1376264 | tf_op jit(solution)/shard_map/ppermute | solution.py:259
  7.8 3.4 %collective-permute-start.3 = (bf16[256,1024]{1,0:T(8,128)(2,1)}, bf16[256,1024]{1,0:T(8,128)(2,1)S(1)}, u32[]{:S(2)}, u32[]{:S(2)}) collective-permute-start(bf16[256,1024]{1,0:T(8,128)(2,1)} %wo0.3), channel_id=1, source_target_pairs={{0,2},{1,3},{2,0},{3,1},{4,6},{5,7},{6,4},{7,5},{8,10},{9,11},{10,... | collective-permute-start | bytes 1572872 | tf_op jit(solution)/shard_map/ppermute | solution.py:259
  11.3 0.0 copy-start.12
  11.3 0.0 copy-start.13
  11.3 0.0 copy-start.14
  11.3 0.0 copy-done.2
  11.3 0.0 copy-done.1
  11.3 0.0 copy-done.8
  11.3 0.0 copy-done.10
  11.3 0.0 copy-done.11
  11.4 0.0 copy-done.15
  11.4 0.0 copy-done.16
  11.4 0.0 copy-done.9
  11.4 0.5 %copy-done.12 = bf16[256]{0:T(256)(128)(2,1)S(1)} copy-done((bf16[256]{0:T(256)(128)(2,1)S(1)}, bf16[256]{0:T(256)(128)(2,1)}, u32[]{:S(2)}) %copy-start.12) | copy-done | bytes 536
  11.9 0.0 copy-done.13
  11.9 0.0 copy-done.14
  12.0 0.0 copy-start.3
  12.0 1.0 %copy-done.3 = bf16[1024,256]{1,0:T(8,128)(2,1)S(1)} copy-done((bf16[1024,256]{1,0:T(8,128)(2,1)S(1)}, bf16[1024,256]{1,0:T(8,128)(2,1)}, u32[]{:S(2)}) %copy-start.3) | copy-done | bytes 524312
  13.0 0.0 copy-start.6
  13.0 1.0 %copy-done.6 = bf16[1,1024,256]{2,1,0:T(8,128)(2,1)S(1)} copy-done((bf16[1,1024,256]{2,1,0:T(8,128)(2,1)S(1)}, bf16[1,1024,256]{2,1,0:T(8,128)(2,1)}, u32[]{:S(2)}) %copy-start.6) | copy-done | bytes 524312
  14.0 0.0 copy-start.7
  14.0 1.8 %own.1 = (bf16[512,256]{1,0:T(8,128)(2,1)S(1)}, f32[512,256]{1,0:T(8,128)S(1)}, f32[512,256]{1,0:T(8,128)S(1)}, s32[128,128]{1,0:T(8,128)S(1)}, f32[8,1024]{1,0:...) custom-call(s32[1,128]{1,0:T(1,128)S(1)} %bitcast.16, s32[1,128]{1,0:T(1,128)S(1)} %copy-done.16, ...), custom_call_target="tpu_custom_call" | custom-call | flops 1024 | bytes 1024 | tf_op jit(solution)/shard_map/own/pallas_call | solution.py:242
  15.8 0.0 copy-done.7
  15.8 7.2 %collective-permute-start.2 = (bf16[256,1024]{1,0:T(8,128)(2,1)S(1)}, bf16[256,1024]{1,0:T(8,128)(2,1)S(1)}, u32[]{:S(2)}, u32[]{:S(2)}) collective-permute-start(bf16[256,1024]{1,0:T(8,128)(2,1)S(1)} %copy-done.7), channel_id=1, source_target_pairs={{0,1},{1,0},{2,3},{3,2},{4,5},{5,4},{6,7},{7,6},{8,9},{9,8},{10,11... | collective-permute-start | bytes 1572872 | tf_op jit(solution)/shard_map/ppermute | solution.py:259
  23.1 0.0 collective-permute-done.k_ref
  23.1 0.9 %peer_score.1 = (bf16[512,896]{1,0:T(8,128)(2,1)S(1)}, f32[512,256]{1,0:T(8,128)S(1)}, f32[512,128]{1,0:T(8,128)S(1)}, bf16[256,896]{1,0:T(8,128)(2,1)S(1)}) custom-call(f32[8,1920]{1,0:T(8,128)S(1)} %get-tuple-element.21.bias_ref, bf16[512,256]{1,0:T(8,128)(2,1)S(1)} %get-tuple-element.22.q_ref, bf16[896,256]{1,0:T(8,128)(2,1)S(1)} %collective-permute-done.k_ref, ...), custom_call_target="tpu_custom_call" | custom-call | flops 8589934592 | bytes 1024 | tf_op jit(solution)/shard_map/peer_score/pallas_call | solution.py:242
  24.0 0.0 collective-permute-done.3.wo2
  24.0 3.9 %collective-permute-start.4 = (bf16[256,1024]{1,0:T(8,128)(2,1)S(1)}, bf16[256,1024]{1,0:T(8,128)(2,1)S(1)}, u32[]{:S(2)}, u32[]{:S(2)}) collective-permute-start(bf16[256,1024]{1,0:T(8,128)(2,1)S(1)} %collective-permute-done.3.wo2), channel_id=1, source_target_pairs={{0,1},{1,0},{2,3},{3,2},{4,5},{5,4},{6,7},{7,6},{8,9},{9,8},{10,11... | collective-permute-start | bytes 1572872 | tf_op jit(solution)/shard_map/ppermute | solution.py:259
  27.9 0.0 collective-permute-done.1.v_ref.pv_ref
  27.9 0.0 copy-start.4
  27.9 0.4 peer_value.1
  28.3 5.9 %all-gather = bf16[512,256]{1,0:T(8,128)(2,1)S(1)} all-gather(bf16[128,256]{1,0:T(8,128)(2,1)S(1)} %peer_value.1), channel_id=2, replica_groups=mesh['group'=128,'tensor'=4] {'tensor'}, dimensions={0}, use_global_device_ids=true | all-gather | bytes 327680 | tf_op jit(solution)/shard_map/all_gather | solution.py:304
  34.2 0.0 collective-permute-done.2.wo1
  34.2 0.0 collective-permute-done.4.wo3
  34.2 0.0 copy-done.4
  34.2 3.2 %second.1 = (bf16[128,1024]{1,0:T(8,128)(2,1)S(1)}, bf16[128,256]{1,0:T(8,128)(2,1)S(1)}) custom-call(f32[8,1920]{1,0:T(8,128)S(1)} %get-tuple-element.21.bias_ref, bf16[4,128,256]{2,1,0:T(8,128)(2,1)S(1)} %bitcast.14, bf16[256,1024]{1,0:T(8,128)(2,1)S(1)} %copy-done.7, bf16[256,1024]{1,0:T(8,128)(2,1)S(1)} %collective-permute-done.2.wo1, ...), custom_call_target="tpu_custom_call" | custom-call | flops 1024 | bytes 1024 | tf_op jit(solution)/shard_map/second/pallas_call | solution.py:242
  37.4 5.9 %all-gather.1 = bf16[512,256]{1,0:T(8,128)(2,1)S(1)} all-gather(bf16[128,256]{1,0:T(8,128)(2,1)S(1)} %get-tuple-element.35), channel_id=3, replica_groups=mesh['group'=128,'tensor'=4] {'tensor'}, dimensions={0}, use_global_device_ids=true | all-gather | bytes 327680 | tf_op jit(solution)/shard_map/all_gather | solution.py:313
  43.3 1.4 %last.1 = bf16[128,1024]{1,0:T(8,128)(2,1)} custom-call(bf16[4,128,256]{2,1,0:T(8,128)(2,1)S(1)} %bitcast.15, bf16[256,1024]{1,0:T(8,128)(2,1)S(1)} %copy-done.7, bf16[256,1024]{1,0:T(8,128)(2,1)S(1)} %collective-permute-done.2.wo1, bf16[256,1024]{1,0:T(8,128)(2,1)S(1)} %collective-permute-done.3.wo2, bf16[256,1024]{1,0:T(8,128)(2,1)S(1)} %collective-permute-done.4.wo3, ...), custom_call_target="tpu_custom_call" | custom-call | flops 1024 | bytes 1024 | tf_op jit(solution)/shard_map/last/pallas_call | solution.py:242
Async XLA Ops:
  0.0 5.5 %copy-start = (bf16[1,1024,256]{2,1,0:T(8,128)(2,1)S(1)}, bf16[1,1024,256]{2,1,0:T(8,128)(2,1)}, u32[]{:S(2)}) copy-start(bf16[1,1024,256]{2,1,0:T(8,128)(2,1)} %param.19) | copy-start | bytes 1572868
  0.0 1.1 %copy-start.5 = (bf16[1,1024,256]{2,1,0:T(8,128)(2,1)S(1)}, bf16[1,1024,256]{2,1,0:T(8,128)(2,1)}, u32[]{:S(2)}) copy-start(bf16[1,1024,256]{2,1,0:T(8,128)(2,1)} %param.18) | copy-start | bytes 1572868
  1.1 10.2 %copy-start.2 = (bf16[1024,256]{1,0:T(8,128)(2,1)S(1)}, bf16[1024,256]{1,0:T(8,128)(2,1)}, u32[]{:S(2)}) copy-start(bf16[1024,256]{1,0:T(8,128)(2,1)} %wk_ref.3) | copy-start | bytes 1572868
  1.4 9.9 %copy-start.1 = (bf16[1024,256]{1,0:T(8,128)(2,1)S(1)}, bf16[1024,256]{1,0:T(8,128)(2,1)}, u32[]{:S(2)}) copy-start(bf16[1024,256]{1,0:T(8,128)(2,1)} %wq_ref.3) | copy-start | bytes 1572868
  1.4 21.7 %collective-permute-start = (bf16[896,256]{1,0:T(8,128)(2,1)S(1)}, bf16[896,256]{1,0:T(8,128)(2,1)S(1)}, u32[]{:S(2)}, u32[]{:S(2)}) collective-permute-start(bf16[896,256]{1,0:T(8,128)(2,1)S(1)} %send_k.1), channel_id=1, source_target_pairs={{0,4},{4,0},{8,12},{12,8},{16,20},{20,16},{24,28},{28,24},{32,36},... | collective-permute-start | bytes 1376264 | tf_op jit(solution)/shard_map/ppermute | solution.py:259
  5.5 5.8 %copy-start.8 = (bf16[1,128,1024]{2,1,0:T(8,128)(2,1)S(1)}, bf16[1,128,1024]{2,1,0:T(8,128)(2,1)}, u32[]{:S(2)}) copy-start(bf16[1,128,1024]{2,1,0:T(8,128)(2,1)} %param.15) | copy-start | bytes 786436
  5.5 5.8 %copy-start.10 = (bf16[1024]{0:T(1024)(128)(2,1)S(1)}, bf16[1024]{0:T(1024)(128)(2,1)}, u32[]{:S(2)}) copy-start(bf16[1024]{0:T(1024)(128)(2,1)} %gain_ref.1) | copy-start | bytes 6148
  5.5 5.8 %copy-start.11 = (bf16[1024]{0:T(1024)(128)(2,1)S(1)}, bf16[1024]{0:T(1024)(128)(2,1)}, u32[]{:S(2)}) copy-start(bf16[1024]{0:T(1024)(128)(2,1)} %shift_ref.1) | copy-start | bytes 6148
  5.5 5.8 %copy-start.15 = (s32[128]{0:T(128)S(1)}, s32[128]{0:T(128)}, u32[]{:S(2)}) copy-start(s32[128]{0:T(128)} %param.17) | copy-start | bytes 1540
  5.5 5.8 %copy-start.16 = (s32[1,128]{1,0:T(1,128)S(1)}, s32[1,128]{1,0:T(1,128)}, u32[]{:S(2)}) copy-start(s32[1,128]{1,0:T(1,128)} %mask_ref.1) | copy-start | bytes 1540
  5.9 5.5 %copy-start.9 = (bf16[1024]{0:T(1024)(128)(2,1)S(1)}, bf16[1024]{0:T(1024)(128)(2,1)}, u32[]{:S(2)}) copy-start(bf16[1024]{0:T(1024)(128)(2,1)} %bo_ref.1) | copy-start | bytes 6148
  5.9 22.0 %collective-permute-start.1 = (bf16[896,256]{1,0:T(8,128)(2,1)S(1)}, bf16[896,256]{1,0:T(8,128)(2,1)S(1)}, u32[]{:S(2)}, u32[]{:S(2)}) collective-permute-start(bf16[896,256]{1,0:T(8,128)(2,1)S(1)} %send_v.1), channel_id=1, source_target_pairs={{0,4},{4,0},{8,12},{12,8},{16,20},{20,16},{24,28},{28,24},{32,36},... | collective-permute-start | bytes 1376264 | tf_op jit(solution)/shard_map/ppermute | solution.py:259
  7.8 16.2 %collective-permute-start.3 = (bf16[256,1024]{1,0:T(8,128)(2,1)}, bf16[256,1024]{1,0:T(8,128)(2,1)S(1)}, u32[]{:S(2)}, u32[]{:S(2)}) collective-permute-start(bf16[256,1024]{1,0:T(8,128)(2,1)} %wo0.3), channel_id=1, source_target_pairs={{0,2},{1,3},{2,0},{3,1},{4,6},{5,7},{6,4},{7,5},{8,10},{9,11},{10,... | collective-permute-start | bytes 1572872 | tf_op jit(solution)/shard_map/ppermute | solution.py:259
  11.3 0.7 %copy-start.12 = (bf16[256]{0:T(256)(128)(2,1)S(1)}, bf16[256]{0:T(256)(128)(2,1)}, u32[]{:S(2)}) copy-start(bf16[256]{0:T(256)(128)(2,1)} %bq_ref.3) | copy-start | bytes 1540
  11.3 0.7 %copy-start.13 = (bf16[256]{0:T(256)(128)(2,1)S(1)}, bf16[256]{0:T(256)(128)(2,1)}, u32[]{:S(2)}) copy-start(bf16[256]{0:T(256)(128)(2,1)} %bk_ref.3) | copy-start | bytes 1540
  11.3 0.7 %copy-start.14 = (bf16[256]{0:T(256)(128)(2,1)S(1)}, bf16[256]{0:T(256)(128)(2,1)}, u32[]{:S(2)}) copy-start(bf16[256]{0:T(256)(128)(2,1)} %bv_ref.3) | copy-start | bytes 1540
  12.0 1.0 %copy-start.3 = (bf16[1024,256]{1,0:T(8,128)(2,1)S(1)}, bf16[1024,256]{1,0:T(8,128)(2,1)}, u32[]{:S(2)}) copy-start(bf16[1024,256]{1,0:T(8,128)(2,1)} %wv_ref.3) | copy-start | bytes 1572868
  13.0 1.0 %copy-start.6 = (bf16[1,1024,256]{2,1,0:T(8,128)(2,1)S(1)}, bf16[1,1024,256]{2,1,0:T(8,128)(2,1)}, u32[]{:S(2)}) copy-start(bf16[1,1024,256]{2,1,0:T(8,128)(2,1)} %param.18) | copy-start | bytes 1572868
  14.0 1.8 %copy-start.7 = (bf16[256,1024]{1,0:T(8,128)(2,1)S(1)}, bf16[256,1024]{1,0:T(8,128)(2,1)}, u32[]{:S(2)}) copy-start(bf16[256,1024]{1,0:T(8,128)(2,1)} %wo0.3) | copy-start | bytes 1572868
  15.8 18.4 %collective-permute-start.2 = (bf16[256,1024]{1,0:T(8,128)(2,1)S(1)}, bf16[256,1024]{1,0:T(8,128)(2,1)S(1)}, u32[]{:S(2)}, u32[]{:S(2)}) collective-permute-start(bf16[256,1024]{1,0:T(8,128)(2,1)S(1)} %copy-done.7), channel_id=1, source_target_pairs={{0,1},{1,0},{2,3},{3,2},{4,5},{5,4},{6,7},{7,6},{8,9},{9,8},{10,11... | collective-permute-start | bytes 1572872 | tf_op jit(solution)/shard_map/ppermute | solution.py:259
  24.0 10.2 %collective-permute-start.4 = (bf16[256,1024]{1,0:T(8,128)(2,1)S(1)}, bf16[256,1024]{1,0:T(8,128)(2,1)S(1)}, u32[]{:S(2)}, u32[]{:S(2)}) collective-permute-start(bf16[256,1024]{1,0:T(8,128)(2,1)S(1)} %collective-permute-done.3.wo2), channel_id=1, source_target_pairs={{0,1},{1,0},{2,3},{3,2},{4,5},{5,4},{6,7},{7,6},{8,9},{9,8},{10,11... | collective-permute-start | bytes 1572872 | tf_op jit(solution)/shard_map/ppermute | solution.py:259
  27.9 6.3 %copy-start.4 = (bf16[1024,256]{1,0:T(8,128)(2,1)S(1)}, bf16[1024,256]{1,0:T(8,128)(2,1)}, u32[]{:S(2)}) copy-start(bf16[1024,256]{1,0:T(8,128)(2,1)} %wv_ref.3) | copy-start | bytes 1572868

commit v4 on v3

--- a/solution.py
+++ b/solution.py
@@ -195,11 +195,12 @@
     rows = second_ref[...]
     stacked = stack_queries(rows, wq_ref, bq_ref)
     own, cached = kt_ref.shape[1], kt_ref.shape[1] + pkt_ref.shape[1]
-    s_ref[:, :own] = mm(stacked, kt_ref[...])
-    s_ref[:, own:cached] = mm(stacked, pkt_ref[...])
     new_k = project(rows, wk_ref, bk_ref)
     new_v = project(rows, wv_ref, bv_ref)
-    s_ref[:, cached:] = mm_t(stacked, new_k)
+    for block in chunks(0, stacked.shape[0], 256):
+        s_ref[block, :own] = mm(stacked[block], kt_ref[...])
+        s_ref[block, own:cached] = mm(stacked[block], pkt_ref[...])
+        s_ref[block, cached:] = mm_t(stacked[block], new_k)
     bias = bias_ref[0:1, :]
     head_of = lax.broadcasted_iota(jnp.int32, att_out_ref.shape, 1) // HD
     merged = jnp.zeros(att_out_ref.shape, F32)
@@ -273,10 +274,11 @@
 
     def sendable(array, name):
         return call(
-            send_kernel, name, shape((slab - SHORTEST, width), BF16), in_hbm=(array,), scratch=[dma]
+            send_kernel, name, shape((slab - SHORTEST, width), BF16), in_hbm=(array,),
+            scratch=[dma],
         )
 
-    send_k = sendable(own_k, "send_k")
+    send_k = sendable(pltpu.with_memory_space_constraint(own_k, pltpu.HBM), "send_k")
     send_v = sendable(after(own_v, send_k), "send_v")
     peer_k = moved(send_k, "group", 1)
     peer_v = moved(send_v, "group", 1)

time: 45.1 us -> 44.6 us (0.989)
  local copies, waits for them, and re-layouts: 3.83 us -> 2.73 us
  Pallas kernels: 8.29 us -> 8.91 us
    unnamed x34 -> x32, local copies, waits for them, and re-layouts: 3.83 us -> 2.73 us
    pallas_call x7, Pallas kernels: 8.29 us -> 8.91 us  [call(): pl.pallas_call(kernel, name=name, out_shape=outs, in_specs=specs, out_spe...]
where the time goes in v4:
time: 44.6 us; the launch traced here: 44.2 us
  starting transfers between devices  20.5 us (46%)
  blocking collectives  11.7 us (26%)
  Pallas kernels  8.91 us (20%)
  local copies, waits for them, and re-layouts  2.73 us (6%)
    ppermute x5, starting transfers between devices, moved(): lax.ppermute(array, axis, [(i, i ^ apart) for i in range(lax.axis_size(ax...  20.5 us
    all_gather x2, blocking collectives, body(): att = lax.all_gather(att, 'tensor')  11.7 us
    pallas_call x7, Pallas kernels, call(): pl.pallas_call(kernel, name=name, out_shape=outs, in_specs=specs, out_spe...  8.91 us
    unnamed x32, local copies, waits for them, and re-layouts  2.73 us
  transfers between devices with their start and end apart: 5, of which 0 were waited for; matrix products, arithmetic and copies ran while one was open for 0% of the time, Pallas kernels for 8%

profile of v4, /device:TPU:1, one launch (start us, length us, event | category | flops | bytes accessed | tf_op | source)
XLA Modules:
  0.0 44.2 jit_solution(4439128586693334287)
XLA Ops:
  0.0 0.0 copy-start
  0.0 0.0 copy-start.2
  0.0 1.1 %send_k.1 = bf16[896,256]{1,0:T(8,128)(2,1)S(1)} custom-call(bf16[1024,256]{1,0:T(8,128)(2,1)} %bitcast.10), custom_call_target="tpu_custom_call" | custom-call | flops 1024 | bytes 1024 | tf_op jit(solution)/shard_map/send_k/pallas_call | solution.py:243
  1.1 0.0 copy-start.1
  1.1 4.1 %collective-permute-start = (bf16[896,256]{1,0:T(8,128)(2,1)S(1)}, bf16[896,256]{1,0:T(8,128)(2,1)S(1)}, u32[]{:S(2)}, u32[]{:S(2)}) collective-permute-start(bf16[896,256]{1,0:T(8,128)(2,1)S(1)} %send_k.1), channel_id=1, source_target_pairs={{0,4},{4,0},{8,12},{12,8},{16,20},{20,16},{24,28},{28,24},{32,36},... | collective-permute-start | bytes 1376264 | tf_op jit(solution)/shard_map/ppermute | solution.py:260
  5.2 0.0 copy-done
  5.2 0.0 copy-start.7
  5.2 0.0 copy-start.9
  5.3 0.0 copy-start.10
  5.3 0.0 copy-start.14
  5.3 0.0 copy-start.15
  5.3 0.3 send_v.1
  5.6 0.0 copy-start.8
  5.6 1.9 %collective-permute-start.1 = (bf16[896,256]{1,0:T(8,128)(2,1)S(1)}, bf16[896,256]{1,0:T(8,128)(2,1)S(1)}, u32[]{:S(2)}, u32[]{:S(2)}) collective-permute-start(bf16[896,256]{1,0:T(8,128)(2,1)S(1)} %send_v.1), channel_id=1, source_target_pairs={{0,4},{4,0},{8,12},{12,8},{16,20},{20,16},{24,28},{28,24},{32,36},... | collective-permute-start | bytes 1376264 | tf_op jit(solution)/shard_map/ppermute | solution.py:260
  7.5 3.4 %collective-permute-start.3 = (bf16[256,1024]{1,0:T(8,128)(2,1)}, bf16[256,1024]{1,0:T(8,128)(2,1)S(1)}, u32[]{:S(2)}, u32[]{:S(2)}) collective-permute-start(bf16[256,1024]{1,0:T(8,128)(2,1)} %wo0.3), channel_id=1, source_target_pairs={{0,2},{1,3},{2,0},{3,1},{4,6},{5,7},{6,4},{7,5},{8,10},{9,11},{10,... | collective-permute-start | bytes 1572872 | tf_op jit(solution)/shard_map/ppermute | solution.py:260
  11.0 0.0 copy-start.11
  11.0 0.0 copy-start.12
  11.0 0.0 copy-start.13
  11.0 0.0 copy-done.2
  11.0 0.0 copy-done.1
  11.1 0.0 copy-done.7
  11.1 0.0 copy-done.9
  11.1 0.0 copy-done.10
  11.1 0.0 copy-done.14
  11.1 0.0 copy-done.15
  11.1 0.0 copy-done.8
  11.1 0.5 %copy-done.11 = bf16[256]{0:T(256)(128)(2,1)S(1)} copy-done((bf16[256]{0:T(256)(128)(2,1)S(1)}, bf16[256]{0:T(256)(128)(2,1)}, u32[]{:S(2)}) %copy-start.11) | copy-done | bytes 536
  11.7 0.0 copy-done.12
  11.7 0.0 copy-done.13
  11.7 0.0 copy-start.3
  11.7 1.0 %copy-done.3 = bf16[1024,256]{1,0:T(8,128)(2,1)S(1)} copy-done((bf16[1024,256]{1,0:T(8,128)(2,1)S(1)}, bf16[1024,256]{1,0:T(8,128)(2,1)}, u32[]{:S(2)}) %copy-start.3) | copy-done | bytes 524312
  12.7 0.0 copy-start.5
  12.7 1.0 %copy-done.5 = bf16[1,1024,256]{2,1,0:T(8,128)(2,1)S(1)} copy-done((bf16[1,1024,256]{2,1,0:T(8,128)(2,1)S(1)}, bf16[1,1024,256]{2,1,0:T(8,128)(2,1)}, u32[]{:S(2)}) %copy-start.5) | copy-done | bytes 524312
  13.8 0.0 copy-start.6
  13.8 1.8 %own.1 = (bf16[512,256]{1,0:T(8,128)(2,1)S(1)}, f32[512,256]{1,0:T(8,128)S(1)}, f32[512,256]{1,0:T(8,128)S(1)}, s32[128,128]{1,0:T(8,128)S(1)}, f32[8,1024]{1,0:...) custom-call(s32[1,128]{1,0:T(1,128)S(1)} %bitcast.16, s32[1,128]{1,0:T(1,128)S(1)} %copy-done.15, ...), custom_call_target="tpu_custom_call" | custom-call | flops 1024 | bytes 1024 | tf_op jit(solution)/shard_map/own/pallas_call | solution.py:243
  15.6 0.0 copy-done.6
  15.6 7.2 %collective-permute-start.2 = (bf16[256,1024]{1,0:T(8,128)(2,1)S(1)}, bf16[256,1024]{1,0:T(8,128)(2,1)S(1)}, u32[]{:S(2)}, u32[]{:S(2)}) collective-permute-start(bf16[256,1024]{1,0:T(8,128)(2,1)S(1)} %copy-done.6), channel_id=1, source_target_pairs={{0,1},{1,0},{2,3},{3,2},{4,5},{5,4},{6,7},{7,6},{8,9},{9,8},{10,11... | collective-permute-start | bytes 1572872 | tf_op jit(solution)/shard_map/ppermute | solution.py:260
  22.8 0.0 collective-permute-done.k_ref
  22.8 0.9 %peer_score.1 = (bf16[512,896]{1,0:T(8,128)(2,1)S(1)}, f32[512,256]{1,0:T(8,128)S(1)}, f32[512,128]{1,0:T(8,128)S(1)}, bf16[256,896]{1,0:T(8,128)(2,1)S(1)}) custom-call(f32[8,1920]{1,0:T(8,128)S(1)} %get-tuple-element.21.bias_ref, bf16[512,256]{1,0:T(8,128)(2,1)S(1)} %get-tuple-element.22.q_ref, bf16[896,256]{1,0:T(8,128)(2,1)S(1)} %collective-permute-done.k_ref, ...), custom_call_target="tpu_custom_call" | custom-call | flops 8589934592 | bytes 1024 | tf_op jit(solution)/shard_map/peer_score/pallas_call | solution.py:243
  23.7 0.0 collective-permute-done.3.wo2
  23.7 3.9 %collective-permute-start.4 = (bf16[256,1024]{1,0:T(8,128)(2,1)S(1)}, bf16[256,1024]{1,0:T(8,128)(2,1)S(1)}, u32[]{:S(2)}, u32[]{:S(2)}) collective-permute-start(bf16[256,1024]{1,0:T(8,128)(2,1)S(1)} %collective-permute-done.3.wo2), channel_id=1, source_target_pairs={{0,1},{1,0},{2,3},{3,2},{4,5},{5,4},{6,7},{7,6},{8,9},{9,8},{10,11... | collective-permute-start | bytes 1572872 | tf_op jit(solution)/shard_map/ppermute | solution.py:260
  27.6 0.0 collective-permute-done.1.v_ref.pv_ref
  27.6 0.0 copy-start.4
  27.6 0.4 %peer_value.1 = bf16[128,256]{1,0:T(8,128)(2,1)S(1)} custom-call(bf16[512,896]{1,0:T(8,128)(2,1)S(1)} %get-tuple-element.25.e_ref, bf16[896,256]{1,0:T(8,128)(2,1)S(1)} %collective-permute-done.1.v_ref.pv_ref, f32[512,256]{1,0:T(8,128)S(1)} %get-tuple-element.27.acc_ref, f32[512,128]{1,0:T(8,128)S(1)} %get-tuple-element.28.scale_ref), custom_call_target="tpu_custom_call" | custom-call | flops 1024 | bytes 1024 | tf_op jit(solution)/shard_map/peer_value/pallas_call | solution.py:243
  28.1 5.9 %all-gather = bf16[512,256]{1,0:T(8,128)(2,1)S(1)} all-gather(bf16[128,256]{1,0:T(8,128)(2,1)S(1)} %peer_value.1), channel_id=2, replica_groups=mesh['group'=128,'tensor'=4] {'tensor'}, dimensions={0}, use_global_device_ids=true | all-gather | bytes 327680 | tf_op jit(solution)/shard_map/all_gather | solution.py:306
  33.9 0.0 collective-permute-done.2.wo1
  33.9 0.0 collective-permute-done.4.wo3
  33.9 0.0 copy-done.4
  33.9 3.0 %second.1 = (bf16[128,1024]{1,0:T(8,128)(2,1)S(1)}, bf16[128,256]{1,0:T(8,128)(2,1)S(1)}) custom-call(f32[8,1920]{1,0:T(8,128)S(1)} %get-tuple-element.21.bias_ref, bf16[4,128,256]{2,1,0:T(8,128)(2,1)S(1)} %bitcast.14, bf16[256,1024]{1,0:T(8,128)(2,1)S(1)} %copy-done.6, bf16[256,1024]{1,0:T(8,128)(2,1)S(1)} %collective-permute-done.2.wo1, ...), custom_call_target="tpu_custom_call" | custom-call | flops 1024 | bytes 1024 | tf_op jit(solution)/shard_map/second/pallas_call | solution.py:243
  36.9 5.9 %all-gather.1 = bf16[512,256]{1,0:T(8,128)(2,1)S(1)} all-gather(bf16[128,256]{1,0:T(8,128)(2,1)S(1)} %get-tuple-element.35), channel_id=3, replica_groups=mesh['group'=128,'tensor'=4] {'tensor'}, dimensions={0}, use_global_device_ids=true | all-gather | bytes 327680 | tf_op jit(solution)/shard_map/all_gather | solution.py:315
  42.8 1.4 %last.1 = bf16[128,1024]{1,0:T(8,128)(2,1)} custom-call(bf16[4,128,256]{2,1,0:T(8,128)(2,1)S(1)} %bitcast.15, bf16[256,1024]{1,0:T(8,128)(2,1)S(1)} %copy-done.6, bf16[256,1024]{1,0:T(8,128)(2,1)S(1)} %collective-permute-done.2.wo1, bf16[256,1024]{1,0:T(8,128)(2,1)S(1)} %collective-permute-done.3.wo2, bf16[256,1024]{1,0:T(8,128)(2,1)S(1)} %collective-permute-done.4.wo3, ...), custom_call_target="tpu_custom_call" | custom-call | flops 1024 | bytes 1024 | tf_op jit(solution)/shard_map/last/pallas_call | solution.py:243
Async XLA Ops:
  0.0 5.2 %copy-start = (bf16[1,1024,256]{2,1,0:T(8,128)(2,1)S(1)}, bf16[1,1024,256]{2,1,0:T(8,128)(2,1)}, u32[]{:S(2)}) copy-start(bf16[1,1024,256]{2,1,0:T(8,128)(2,1)} %param.19) | copy-start | bytes 1572868
  0.0 11.0 %copy-start.2 = (bf16[1024,256]{1,0:T(8,128)(2,1)S(1)}, bf16[1024,256]{1,0:T(8,128)(2,1)}, u32[]{:S(2)}) copy-start(bf16[1024,256]{1,0:T(8,128)(2,1)} %wk_ref.3) | copy-start | bytes 1572868
  1.1 9.9 %copy-start.1 = (bf16[1024,256]{1,0:T(8,128)(2,1)S(1)}, bf16[1024,256]{1,0:T(8,128)(2,1)}, u32[]{:S(2)}) copy-start(bf16[1024,256]{1,0:T(8,128)(2,1)} %wq_ref.3) | copy-start | bytes 1572868
  1.1 21.7 %collective-permute-start = (bf16[896,256]{1,0:T(8,128)(2,1)S(1)}, bf16[896,256]{1,0:T(8,128)(2,1)S(1)}, u32[]{:S(2)}, u32[]{:S(2)}) collective-permute-start(bf16[896,256]{1,0:T(8,128)(2,1)S(1)} %send_k.1), channel_id=1, source_target_pairs={{0,4},{4,0},{8,12},{12,8},{16,20},{20,16},{24,28},{28,24},{32,36},... | collective-permute-start | bytes 1376264 | tf_op jit(solution)/shard_map/ppermute | solution.py:260
  5.2 5.8 %copy-start.7 = (bf16[1,128,1024]{2,1,0:T(8,128)(2,1)S(1)}, bf16[1,128,1024]{2,1,0:T(8,128)(2,1)}, u32[]{:S(2)}) copy-start(bf16[1,128,1024]{2,1,0:T(8,128)(2,1)} %param.15) | copy-start | bytes 786436
  5.2 5.8 %copy-start.9 = (bf16[1024]{0:T(1024)(128)(2,1)S(1)}, bf16[1024]{0:T(1024)(128)(2,1)}, u32[]{:S(2)}) copy-start(bf16[1024]{0:T(1024)(128)(2,1)} %gain_ref.1) | copy-start | bytes 6148
  5.3 5.8 %copy-start.10 = (bf16[1024]{0:T(1024)(128)(2,1)S(1)}, bf16[1024]{0:T(1024)(128)(2,1)}, u32[]{:S(2)}) copy-start(bf16[1024]{0:T(1024)(128)(2,1)} %shift_ref.1) | copy-start | bytes 6148
  5.3 5.8 %copy-start.14 = (s32[128]{0:T(128)S(1)}, s32[128]{0:T(128)}, u32[]{:S(2)}) copy-start(s32[128]{0:T(128)} %param.17) | copy-start | bytes 1540
  5.3 5.8 %copy-start.15 = (s32[1,128]{1,0:T(1,128)S(1)}, s32[1,128]{1,0:T(1,128)}, u32[]{:S(2)}) copy-start(s32[1,128]{1,0:T(1,128)} %mask_ref.1) | copy-start | bytes 1540
  5.6 5.5 %copy-start.8 = (bf16[1024]{0:T(1024)(128)(2,1)S(1)}, bf16[1024]{0:T(1024)(128)(2,1)}, u32[]{:S(2)}) copy-start(bf16[1024]{0:T(1024)(128)(2,1)} %bo_ref.1) | copy-start | bytes 6148
  5.6 22.0 %collective-permute-start.1 = (bf16[896,256]{1,0:T(8,128)(2,1)S(1)}, bf16[896,256]{1,0:T(8,128)(2,1)S(1)}, u32[]{:S(2)}, u32[]{:S(2)}) collective-permute-start(bf16[896,256]{1,0:T(8,128)(2,1)S(1)} %send_v.1), channel_id=1, source_target_pairs={{0,4},{4,0},{8,12},{12,8},{16,20},{20,16},{24,28},{28,24},{32,36},... | collective-permute-start | bytes 1376264 | tf_op jit(solution)/shard_map/ppermute | solution.py:260
  7.5 16.2 %collective-permute-start.3 = (bf16[256,1024]{1,0:T(8,128)(2,1)}, bf16[256,1024]{1,0:T(8,128)(2,1)S(1)}, u32[]{:S(2)}, u32[]{:S(2)}) collective-permute-start(bf16[256,1024]{1,0:T(8,128)(2,1)} %wo0.3), channel_id=1, source_target_pairs={{0,2},{1,3},{2,0},{3,1},{4,6},{5,7},{6,4},{7,5},{8,10},{9,11},{10,... | collective-permute-start | bytes 1572872 | tf_op jit(solution)/shard_map/ppermute | solution.py:260
  11.0 0.7 %copy-start.11 = (bf16[256]{0:T(256)(128)(2,1)S(1)}, bf16[256]{0:T(256)(128)(2,1)}, u32[]{:S(2)}) copy-start(bf16[256]{0:T(256)(128)(2,1)} %bq_ref.3) | copy-start | bytes 1540
  11.0 0.7 %copy-start.12 = (bf16[256]{0:T(256)(128)(2,1)S(1)}, bf16[256]{0:T(256)(128)(2,1)}, u32[]{:S(2)}) copy-start(bf16[256]{0:T(256)(128)(2,1)} %bk_ref.3) | copy-start | bytes 1540
  11.0 0.7 %copy-start.13 = (bf16[256]{0:T(256)(128)(2,1)S(1)}, bf16[256]{0:T(256)(128)(2,1)}, u32[]{:S(2)}) copy-start(bf16[256]{0:T(256)(128)(2,1)} %bv_ref.3) | copy-start | bytes 1540
  11.7 1.0 %copy-start.3 = (bf16[1024,256]{1,0:T(8,128)(2,1)S(1)}, bf16[1024,256]{1,0:T(8,128)(2,1)}, u32[]{:S(2)}) copy-start(bf16[1024,256]{1,0:T(8,128)(2,1)} %wv_ref.3) | copy-start | bytes 1572868
  12.7 1.0 %copy-start.5 = (bf16[1,1024,256]{2,1,0:T(8,128)(2,1)S(1)}, bf16[1,1024,256]{2,1,0:T(8,128)(2,1)}, u32[]{:S(2)}) copy-start(bf16[1,1024,256]{2,1,0:T(8,128)(2,1)} %param.18) | copy-start | bytes 1572868
  13.8 1.8 %copy-start.6 = (bf16[256,1024]{1,0:T(8,128)(2,1)S(1)}, bf16[256,1024]{1,0:T(8,128)(2,1)}, u32[]{:S(2)}) copy-start(bf16[256,1024]{1,0:T(8,128)(2,1)} %wo0.3) | copy-start | bytes 1572868
  15.6 18.4 %collective-permute-start.2 = (bf16[256,1024]{1,0:T(8,128)(2,1)S(1)}, bf16[256,1024]{1,0:T(8,128)(2,1)S(1)}, u32[]{:S(2)}, u32[]{:S(2)}) collective-permute-start(bf16[256,1024]{1,0:T(8,128)(2,1)S(1)} %copy-done.6), channel_id=1, source_target_pairs={{0,1},{1,0},{2,3},{3,2},{4,5},{5,4},{6,7},{7,6},{8,9},{9,8},{10,11... | collective-permute-start | bytes 1572872 | tf_op jit(solution)/shard_map/ppermute | solution.py:260
  23.7 10.2 %collective-permute-start.4 = (bf16[256,1024]{1,0:T(8,128)(2,1)S(1)}, bf16[256,1024]{1,0:T(8,128)(2,1)S(1)}, u32[]{:S(2)}, u32[]{:S(2)}) collective-permute-start(bf16[256,1024]{1,0:T(8,128)(2,1)S(1)} %collective-permute-done.3.wo2), channel_id=1, source_target_pairs={{0,1},{1,0},{2,3},{3,2},{4,5},{5,4},{6,7},{7,6},{8,9},{9,8},{10,11... | collective-permute-start | bytes 1572872 | tf_op jit(solution)/shard_map/ppermute | solution.py:260
  27.6 6.3 %copy-start.4 = (bf16[1024,256]{1,0:T(8,128)(2,1)S(1)}, bf16[1024,256]{1,0:T(8,128)(2,1)}, u32[]{:S(2)}) copy-start(bf16[1024,256]{1,0:T(8,128)(2,1)} %wv_ref.3) | copy-start | bytes 1572868

commit v5 on v4

--- a/solution.py
+++ b/solution.py
@@ -143,9 +143,12 @@
 def peer_score_kernel(
     bias_ref, q_ref, k_ref, acc_ref, stat_ref, e_ref, out_ref, scale_ref, kt_ref, s_ref, peer_ref
 ):
-    kept = k_ref.shape[0]
+    kept = kt_ref.shape[1]
     half = stat_ref.shape[1] // 2
-    kt_ref[...] = k_ref[...].T
+    first = pl.multiple_of(
+        jnp.where(lax.axis_index("group") % 2 == 0, 0, k_ref.shape[0] - kept), SHORTEST
+    )
+    kt_ref[...] = k_ref[pl.ds(first, kept), :].T
     bias = bias_ref[0:1, bias_ref.shape[1] - kept :]
     s_ref[...] = mm(q_ref[...], kt_ref[...])
     for at in chunks(0, q_ref.shape[0], STEP):
@@ -278,9 +281,8 @@
             scratch=[dma],
         )
 
-    send_k = sendable(pltpu.with_memory_space_constraint(own_k, pltpu.HBM), "send_k")
-    send_v = sendable(after(own_v, send_k), "send_v")
-    peer_k = moved(send_k, "group", 1)
+    send_v = sendable(own_v, "send_v")
+    peer_k = moved(own_k, "group", 1)
     peer_v = moved(send_v, "group", 1)
     wo2 = moved(w_o, "tensor", 2)
     q_stack, acc, stats, picked, norm, bias, own_kt = call(

time: 44.6 us -> 45.4 us (1.018)
  local copies, waits for them, and re-layouts: 2.73 us -> 5.85 us
  starting transfers between devices: 20.5 us -> 18.5 us
  Pallas kernels: 8.91 us -> 7.82 us
  blocking collectives: 11.7 us -> 12.5 us
    unnamed x32 -> x38, local copies, waits for them, and re-layouts: 2.73 us -> 5.85 us
    ppermute x5, starting transfers between devices: 20.5 us -> 18.5 us  [moved(): lax.ppermute(array, axis, [(i, i ^ apart) for i in range(lax.axis_size(ax...]
    pallas_call x7 -> x6, Pallas kernels: 8.91 us -> 7.82 us  [call(): pl.pallas_call(kernel, name=name, out_shape=outs, in_specs=specs, out_spe...]
    all_gather x2, blocking collectives: 11.7 us -> 12.5 us  [body(): att = lax.all_gather(att, 'tensor')]
where the time goes in v5:
time: 45.4 us; the launch traced here: 44.9 us
  starting transfers between devices  18.5 us (41%)
  blocking collectives  12.5 us (28%)
  Pallas kernels  7.82 us (17%)
  local copies, waits for them, and re-layouts  5.85 us (13%)
    ppermute x5, starting transfers between devices, moved(): lax.ppermute(array, axis, [(i, i ^ apart) for i in range(lax.axis_size(ax...  18.5 us
    all_gather x2, blocking collectives, body(): att = lax.all_gather(att, 'tensor')  12.5 us
    pallas_call x6, Pallas kernels, call(): pl.pallas_call(kernel, name=name, out_shape=outs, in_specs=specs, out_spe...  7.82 us
    unnamed x38, local copies, waits for them, and re-layouts  5.85 us
  transfers between devices with their start and end apart: 5, of which 0 were waited for; matrix products, arithmetic and copies ran while one was open for 0% of the time, Pallas kernels for 8%

profile of v5, /device:TPU:1, one launch (start us, length us, event | category | flops | bytes accessed | tf_op | source)
XLA Modules:
  0.0 44.9 jit_solution(17690093130810545231)
XLA Ops:
  0.0 3.9 %collective-permute-start = (bf16[1024,256]{1,0:T(8,128)(2,1)}, bf16[1024,256]{1,0:T(8,128)(2,1)S(1)}, u32[]{:S(2)}, u32[]{:S(2)}) collective-permute-start(bf16[1024,256]{1,0:T(8,128)(2,1)} %bitcast.14), channel_id=1, source_target_pairs={{0,4},{4,0},{8,12},{12,8},{16,20},{20,16},{24,28},{28,24},{32,36},... | collective-permute-start | bytes 1572872 | tf_op jit(solution)/shard_map/ppermute | solution.py:263
  3.9 0.0 copy-start
  4.0 1.0 %copy-done = bf16[1,1024,256]{2,1,0:T(8,128)(2,1)S(1)} copy-done((bf16[1,1024,256]{2,1,0:T(8,128)(2,1)S(1)}, bf16[1,1024,256]{2,1,0:T(8,128)(2,1)}, u32[]{:S(2)}) %copy-start) | copy-done | bytes 524312
  5.0 0.0 copy-start.1
  5.0 0.0 copy-start.9
  5.0 0.0 copy-start.12
  5.0 0.0 copy-start.13
  5.0 0.0 copy-start.17
  5.0 0.0 copy-start.18
  5.0 0.3 send_v.1
  5.3 0.0 copy-start.11
  5.3 1.9 %collective-permute-start.1 = (bf16[896,256]{1,0:T(8,128)(2,1)S(1)}, bf16[896,256]{1,0:T(8,128)(2,1)S(1)}, u32[]{:S(2)}, u32[]{:S(2)}) collective-permute-start(bf16[896,256]{1,0:T(8,128)(2,1)S(1)} %send_v.1), channel_id=1, source_target_pairs={{0,4},{4,0},{8,12},{12,8},{16,20},{20,16},{24,28},{28,24},{32,36},... | collective-permute-start | bytes 1376264 | tf_op jit(solution)/shard_map/ppermute | solution.py:263
  7.3 3.4 %collective-permute-start.3 = (bf16[256,1024]{1,0:T(8,128)(2,1)}, bf16[256,1024]{1,0:T(8,128)(2,1)S(1)}, u32[]{:S(2)}, u32[]{:S(2)}) collective-permute-start(bf16[256,1024]{1,0:T(8,128)(2,1)} %wo0.3), channel_id=1, source_target_pairs={{0,2},{1,3},{2,0},{3,1},{4,6},{5,7},{6,4},{7,5},{8,10},{9,11},{10,... | collective-permute-start | bytes 1572872 | tf_op jit(solution)/shard_map/ppermute | solution.py:263
  10.7 0.0 copy-start.14
  10.7 0.0 copy-start.15
  10.8 0.0 copy-start.16
  10.8 0.0 copy-done.1
  10.8 0.0 copy-done.9
  10.8 0.0 copy-done.12
  10.8 0.0 copy-done.13
  10.8 0.0 copy-done.17
  10.8 0.0 copy-done.18
  10.8 0.0 copy-done.11
  10.8 0.6 %copy-done.14 = bf16[256]{0:T(256)(128)(2,1)S(1)} copy-done((bf16[256]{0:T(256)(128)(2,1)S(1)}, bf16[256]{0:T(256)(128)(2,1)}, u32[]{:S(2)}) %copy-start.14) | copy-done | bytes 536
  11.4 0.0 copy-done.15
  11.4 0.0 copy-done.16
  11.4 0.0 copy-start.2
  11.4 1.0 %copy-done.2 = bf16[1024,256]{1,0:T(8,128)(2,1)S(1)} copy-done((bf16[1024,256]{1,0:T(8,128)(2,1)S(1)}, bf16[1024,256]{1,0:T(8,128)(2,1)}, u32[]{:S(2)}) %copy-start.2) | copy-done | bytes 524312
  12.5 0.0 copy-start.4
  12.5 1.0 %copy-done.4 = bf16[1024,256]{1,0:T(8,128)(2,1)S(1)} copy-done((bf16[1024,256]{1,0:T(8,128)(2,1)S(1)}, bf16[1024,256]{1,0:T(8,128)(2,1)}, u32[]{:S(2)}) %copy-start.4) | copy-done | bytes 524312
  13.5 0.0 copy-start.6
  13.5 1.0 %copy-done.6 = bf16[1024,256]{1,0:T(8,128)(2,1)S(1)} copy-done((bf16[1024,256]{1,0:T(8,128)(2,1)S(1)}, bf16[1024,256]{1,0:T(8,128)(2,1)}, u32[]{:S(2)}) %copy-start.6) | copy-done | bytes 524312
  14.5 0.0 copy-start.10
  14.5 1.0 %copy-done.10 = bf16[1,1024,256]{2,1,0:T(8,128)(2,1)S(1)} copy-done((bf16[1,1024,256]{2,1,0:T(8,128)(2,1)S(1)}, bf16[1,1024,256]{2,1,0:T(8,128)(2,1)}, u32[]{:S(2)}) %copy-start.10) | copy-done | bytes 524312
  15.6 0.0 copy-start.8
  15.6 1.8 %own.1 = (bf16[512,256]{1,0:T(8,128)(2,1)S(1)}, f32[512,256]{1,0:T(8,128)S(1)}, f32[512,256]{1,0:T(8,128)S(1)}, s32[128,128]{1,0:T(8,128)S(1)}, f32[8,1024]{1,0:...) custom-call(s32[1,128]{1,0:T(1,128)S(1)} %bitcast.16, s32[1,128]{1,0:T(1,128)S(1)} %copy-done.18, ...), custom_call_target="tpu_custom_call" | custom-call | flops 1024 | bytes 1024 | tf_op jit(solution)/shard_map/own/pallas_call | solution.py:246
  17.4 0.0 copy-done.8
  17.4 7.2 %collective-permute-start.2 = (bf16[256,1024]{1,0:T(8,128)(2,1)S(1)}, bf16[256,1024]{1,0:T(8,128)(2,1)S(1)}, u32[]{:S(2)}, u32[]{:S(2)}) collective-permute-start(bf16[256,1024]{1,0:T(8,128)(2,1)S(1)} %copy-done.8), channel_id=1, source_target_pairs={{0,1},{1,0},{2,3},{3,2},{4,5},{5,4},{6,7},{7,6},{8,9},{9,8},{10,11... | collective-permute-start | bytes 1572872 | tf_op jit(solution)/shard_map/ppermute | solution.py:263
  24.6 0.0 collective-permute-done.k_ref
  24.6 0.9 %peer_score.1 = (bf16[512,896]{1,0:T(8,128)(2,1)S(1)}, f32[512,256]{1,0:T(8,128)S(1)}, f32[512,128]{1,0:T(8,128)S(1)}, bf16[256,896]{1,0:T(8,128)(2,1)S(1)}) custom-call(f32[8,1920]{1,0:T(8,128)S(1)} %get-tuple-element.20.bias_ref, bf16[512,256]{1,0:T(8,128)(2,1)S(1)} %get-tuple-element.21.q_ref, bf16[1024,256]{1,0:T(8,128)(2,1)S(1)} %collective-permute-done.k_ref, ...), custom_call_target="tpu_custom_call" | custom-call | flops 8589934592 | bytes 1024 | tf_op jit(solution)/shard_map/peer_score/pallas_call | solution.py:246
  25.6 0.0 collective-permute-done.3.wo2
  25.6 1.9 %collective-permute-start.4 = (bf16[256,1024]{1,0:T(8,128)(2,1)S(1)}, bf16[256,1024]{1,0:T(8,128)(2,1)S(1)}, u32[]{:S(2)}, u32[]{:S(2)}) collective-permute-start(bf16[256,1024]{1,0:T(8,128)(2,1)S(1)} %collective-permute-done.3.wo2), channel_id=1, source_target_pairs={{0,1},{1,0},{2,3},{3,2},{4,5},{5,4},{6,7},{7,6},{8,9},{9,8},{10,11... | collective-permute-start | bytes 1572872 | tf_op jit(solution)/shard_map/ppermute | solution.py:263
  27.5 0.0 collective-permute-done.1.v_ref.pv_ref
  27.5 0.0 copy-start.3
  27.5 0.0 copy-start.5
  27.5 0.0 copy-start.7
  27.5 0.4 peer_value.1
  28.0 6.6 %all-gather = bf16[512,256]{1,0:T(8,128)(2,1)S(1)} all-gather(bf16[128,256]{1,0:T(8,128)(2,1)S(1)} %peer_value.1), channel_id=2, replica_groups=mesh['group'=128,'tensor'=4] {'tensor'}, dimensions={0}, use_global_device_ids=true | all-gather | bytes 327680 | tf_op jit(solution)/shard_map/all_gather | solution.py:308
  34.6 0.0 collective-permute-done.2.wo1
  34.6 0.0 collective-permute-done.4.wo3
  34.6 0.0 copy-done.3
  34.6 0.0 copy-done.5
  34.6 0.0 copy-done.7
  34.6 3.0 %second.1 = (bf16[128,1024]{1,0:T(8,128)(2,1)S(1)}, bf16[128,256]{1,0:T(8,128)(2,1)S(1)}) custom-call(f32[8,1920]{1,0:T(8,128)S(1)} %get-tuple-element.20.bias_ref, bf16[4,128,256]{2,1,0:T(8,128)(2,1)S(1)} %bitcast.12, bf16[256,1024]{1,0:T(8,128)(2,1)S(1)} %copy-done.8, bf16[256,1024]{1,0:T(8,128)(2,1)S(1)} %collective-permute-done.2.wo1, ...), custom_call_target="tpu_custom_call" | custom-call | flops 1024 | bytes 1024 | tf_op jit(solution)/shard_map/second/pallas_call | solution.py:246
  37.6 5.9 %all-gather.1 = bf16[512,256]{1,0:T(8,128)(2,1)S(1)} all-gather(bf16[128,256]{1,0:T(8,128)(2,1)S(1)} %get-tuple-element.33), channel_id=3, replica_groups=mesh['group'=128,'tensor'=4] {'tensor'}, dimensions={0}, use_global_device_ids=true | all-gather | bytes 327680 | tf_op jit(solution)/shard_map/all_gather | solution.py:317
  43.5 1.4 %last.1 = bf16[128,1024]{1,0:T(8,128)(2,1)} custom-call(bf16[4,128,256]{2,1,0:T(8,128)(2,1)S(1)} %bitcast.13, bf16[256,1024]{1,0:T(8,128)(2,1)S(1)} %copy-done.8, bf16[256,1024]{1,0:T(8,128)(2,1)S(1)} %collective-permute-done.2.wo1, bf16[256,1024]{1,0:T(8,128)(2,1)S(1)} %collective-permute-done.3.wo2, bf16[256,1024]{1,0:T(8,128)(2,1)S(1)} %collective-permute-done.4.wo3, ...), custom_call_target="tpu_custom_call" | custom-call | flops 1024 | bytes 1024 | tf_op jit(solution)/shard_map/last/pallas_call | solution.py:246
Async XLA Ops:
  0.0 24.6 %collective-permute-start = (bf16[1024,256]{1,0:T(8,128)(2,1)}, bf16[1024,256]{1,0:T(8,128)(2,1)S(1)}, u32[]{:S(2)}, u32[]{:S(2)}) collective-permute-start(bf16[1024,256]{1,0:T(8,128)(2,1)} %bitcast.14), channel_id=1, source_target_pairs={{0,4},{4,0},{8,12},{12,8},{16,20},{20,16},{24,28},{28,24},{32,36},... | collective-permute-start | bytes 1572872 | tf_op jit(solution)/shard_map/ppermute | solution.py:263
  3.9 1.0 %copy-start = (bf16[1,1024,256]{2,1,0:T(8,128)(2,1)S(1)}, bf16[1,1024,256]{2,1,0:T(8,128)(2,1)}, u32[]{:S(2)}) copy-start(bf16[1,1024,256]{2,1,0:T(8,128)(2,1)} %param.19) | copy-start | bytes 1572868
  5.0 5.8 %copy-start.1 = (bf16[1,1024,256]{2,1,0:T(8,128)(2,1)S(1)}, bf16[1,1024,256]{2,1,0:T(8,128)(2,1)}, u32[]{:S(2)}) copy-start(bf16[1,1024,256]{2,1,0:T(8,128)(2,1)} %param.19) | copy-start | bytes 1572868
  5.0 5.8 %copy-start.9 = (bf16[1,128,1024]{2,1,0:T(8,128)(2,1)S(1)}, bf16[1,128,1024]{2,1,0:T(8,128)(2,1)}, u32[]{:S(2)}) copy-start(bf16[1,128,1024]{2,1,0:T(8,128)(2,1)} %param.15) | copy-start | bytes 786436
  5.0 5.8 %copy-start.12 = (bf16[1024]{0:T(1024)(128)(2,1)S(1)}, bf16[1024]{0:T(1024)(128)(2,1)}, u32[]{:S(2)}) copy-start(bf16[1024]{0:T(1024)(128)(2,1)} %gain_ref.1) | copy-start | bytes 6148
  5.0 5.8 %copy-start.13 = (bf16[1024]{0:T(1024)(128)(2,1)S(1)}, bf16[1024]{0:T(1024)(128)(2,1)}, u32[]{:S(2)}) copy-start(bf16[1024]{0:T(1024)(128)(2,1)} %shift_ref.1) | copy-start | bytes 6148
  5.0 5.8 %copy-start.17 = (s32[128]{0:T(128)S(1)}, s32[128]{0:T(128)}, u32[]{:S(2)}) copy-start(s32[128]{0:T(128)} %param.17) | copy-start | bytes 1540
  5.0 5.8 %copy-start.18 = (s32[1,128]{1,0:T(1,128)S(1)}, s32[1,128]{1,0:T(1,128)}, u32[]{:S(2)}) copy-start(s32[1,128]{1,0:T(1,128)} %mask_ref.1) | copy-start | bytes 1540
  5.3 5.5 %copy-start.11 = (bf16[1024]{0:T(1024)(128)(2,1)S(1)}, bf16[1024]{0:T(1024)(128)(2,1)}, u32[]{:S(2)}) copy-start(bf16[1024]{0:T(1024)(128)(2,1)} %bo_ref.1) | copy-start | bytes 6148
  5.3 22.2 %collective-permute-start.1 = (bf16[896,256]{1,0:T(8,128)(2,1)S(1)}, bf16[896,256]{1,0:T(8,128)(2,1)S(1)}, u32[]{:S(2)}, u32[]{:S(2)}) collective-permute-start(bf16[896,256]{1,0:T(8,128)(2,1)S(1)} %send_v.1), channel_id=1, source_target_pairs={{0,4},{4,0},{8,12},{12,8},{16,20},{20,16},{24,28},{28,24},{32,36},... | collective-permute-start | bytes 1376264 | tf_op jit(solution)/shard_map/ppermute | solution.py:263
  7.3 18.3 %collective-permute-start.3 = (bf16[256,1024]{1,0:T(8,128)(2,1)}, bf16[256,1024]{1,0:T(8,128)(2,1)S(1)}, u32[]{:S(2)}, u32[]{:S(2)}) collective-permute-start(bf16[256,1024]{1,0:T(8,128)(2,1)} %wo0.3), channel_id=1, source_target_pairs={{0,2},{1,3},{2,0},{3,1},{4,6},{5,7},{6,4},{7,5},{8,10},{9,11},{10,... | collective-permute-start | bytes 1572872 | tf_op jit(solution)/shard_map/ppermute | solution.py:263
  10.7 0.7 %copy-start.14 = (bf16[256]{0:T(256)(128)(2,1)S(1)}, bf16[256]{0:T(256)(128)(2,1)}, u32[]{:S(2)}) copy-start(bf16[256]{0:T(256)(128)(2,1)} %bq_ref.3) | copy-start | bytes 1540
  10.7 0.7 %copy-start.15 = (bf16[256]{0:T(256)(128)(2,1)S(1)}, bf16[256]{0:T(256)(128)(2,1)}, u32[]{:S(2)}) copy-start(bf16[256]{0:T(256)(128)(2,1)} %bk_ref.3) | copy-start | bytes 1540
  10.8 0.7 %copy-start.16 = (bf16[256]{0:T(256)(128)(2,1)S(1)}, bf16[256]{0:T(256)(128)(2,1)}, u32[]{:S(2)}) copy-start(bf16[256]{0:T(256)(128)(2,1)} %bv_ref.3) | copy-start | bytes 1540
  11.4 1.0 %copy-start.2 = (bf16[1024,256]{1,0:T(8,128)(2,1)S(1)}, bf16[1024,256]{1,0:T(8,128)(2,1)}, u32[]{:S(2)}) copy-start(bf16[1024,256]{1,0:T(8,128)(2,1)} %wq_ref.3) | copy-start | bytes 1572868
  12.5 1.0 %copy-start.4 = (bf16[1024,256]{1,0:T(8,128)(2,1)S(1)}, bf16[1024,256]{1,0:T(8,128)(2,1)}, u32[]{:S(2)}) copy-start(bf16[1024,256]{1,0:T(8,128)(2,1)} %wk_ref.3) | copy-start | bytes 1572868
  13.5 1.0 %copy-start.6 = (bf16[1024,256]{1,0:T(8,128)(2,1)S(1)}, bf16[1024,256]{1,0:T(8,128)(2,1)}, u32[]{:S(2)}) copy-start(bf16[1024,256]{1,0:T(8,128)(2,1)} %wv_ref.3) | copy-start | bytes 1572868
  14.5 1.0 %copy-start.10 = (bf16[1,1024,256]{2,1,0:T(8,128)(2,1)S(1)}, bf16[1,1024,256]{2,1,0:T(8,128)(2,1)}, u32[]{:S(2)}) copy-start(bf16[1,1024,256]{2,1,0:T(8,128)(2,1)} %param.18) | copy-start | bytes 1572868
  15.6 1.8 %copy-start.8 = (bf16[256,1024]{1,0:T(8,128)(2,1)S(1)}, bf16[256,1024]{1,0:T(8,128)(2,1)}, u32[]{:S(2)}) copy-start(bf16[256,1024]{1,0:T(8,128)(2,1)} %wo0.3) | copy-start | bytes 1572868
  17.4 17.2 %collective-permute-start.2 = (bf16[256,1024]{1,0:T(8,128)(2,1)S(1)}, bf16[256,1024]{1,0:T(8,128)(2,1)S(1)}, u32[]{:S(2)}, u32[]{:S(2)}) collective-permute-start(bf16[256,1024]{1,0:T(8,128)(2,1)S(1)} %copy-done.8), channel_id=1, source_target_pairs={{0,1},{1,0},{2,3},{3,2},{4,5},{5,4},{6,7},{7,6},{8,9},{9,8},{10,11... | collective-permute-start | bytes 1572872 | tf_op jit(solution)/shard_map/ppermute | solution.py:263
  25.6 9.0 %collective-permute-start.4 = (bf16[256,1024]{1,0:T(8,128)(2,1)S(1)}, bf16[256,1024]{1,0:T(8,128)(2,1)S(1)}, u32[]{:S(2)}, u32[]{:S(2)}) collective-permute-start(bf16[256,1024]{1,0:T(8,128)(2,1)S(1)} %collective-permute-done.3.wo2), channel_id=1, source_target_pairs={{0,1},{1,0},{2,3},{3,2},{4,5},{5,4},{6,7},{7,6},{8,9},{9,8},{10,11... | collective-permute-start | bytes 1572872 | tf_op jit(solution)/shard_map/ppermute | solution.py:263
  27.5 7.1 %copy-start.3 = (bf16[1024,256]{1,0:T(8,128)(2,1)S(1)}, bf16[1024,256]{1,0:T(8,128)(2,1)}, u32[]{:S(2)}) copy-start(bf16[1024,256]{1,0:T(8,128)(2,1)} %wq_ref.3) | copy-start | bytes 1572868
  27.5 7.1 %copy-start.5 = (bf16[1024,256]{1,0:T(8,128)(2,1)S(1)}, bf16[1024,256]{1,0:T(8,128)(2,1)}, u32[]{:S(2)}) copy-start(bf16[1024,256]{1,0:T(8,128)(2,1)} %wk_ref.3) | copy-start | bytes 1572868
  27.5 7.1 %copy-start.7 = (bf16[1024,256]{1,0:T(8,128)(2,1)S(1)}, bf16[1024,256]{1,0:T(8,128)(2,1)}, u32[]{:S(2)}) copy-start(bf16[1024,256]{1,0:T(8,128)(2,1)} %wv_ref.3) | copy-start | bytes 1572868
